TPU v7x, 128 devices: a whole 4x4x4 slice. The times are simulated.
128 devices in a mesh: lon: 16 (over z, x_lo, core), lat: 8 (over x_hi, y).
Axes of the slice: x: 4 (x_hi: 2, x_lo: 2; x = x_hi * 2 + x_lo), y: 4, z: 4, core: 2. Of those that a mesh axis runs over, the one named last changes fastest.
Arguments:
- ocean_seed: float32 [4, 10, 1024, 4096], P(None, None, 'lat', 'lon'), may hold values from -6 to 6
- forcing_pert: float32 [4, 256, 2048], P(None, 'lat', 'lon'), may hold values from -6 to 6
- land_mask: int32 [1024, 4096], P('lat', 'lon'), may hold values 0 or 1
- east_coef: float32 [1024, 4096], P('lat', 'lon'), may hold values from 0.02 to 0.2
- north_coef: float32 [1024, 4096], P('lat', 'lon'), may hold values from 0.02 to 0.2
- vert_coef: float32 [9], replicated, may hold values from 0.05 to 0.2
- remap_weight: float32 [2, 1024, 4096], P(None, 'lat', 'lon'), may hold values from 0.1 to 0.9
- ocean_slots: int32 [2, 1024, 4096], P(None, 'lat', 'lon'), may hold values from 0 to 4351, as said below
- serve_cells: int32 [8, 69632], P('lat', 'lon'), may hold values from 0 to 4095, as said below
- fold_map: int32 [4096], replicated, may hold values from 0 to 4095, as said below
Outputs:
- ocean_adjoint: float32 [4, 10, 1024, 4096], P(None, None, 'lat', 'lon')
- stress_sens: float32 [4, 256, 2048], P(None, 'lat', 'lon')
Inputs may be any that keep to these rules, and one draw needn't show every extreme that they name: `ocean_slots`: a slot q < 128 is used only by ocean tiles with a > 0, a slot q >= 4224 only by tiles with a < 7. `serve_cells`: in each list, slots 0 to 127 hold cells of the band's first forcing row, slots 128 + 4096 to 4351 cells of its last forcing row. fold_map[x] = (S - 1 - x) mod 4096 for one S that is a multiple of 256.
All inputs are finite; a program needn't handle non-finite values. No bound on the sum of `land_mask` on one device may be relied on, other than what follows from the above.
Results may differ from a plain program's by a relative error of at most 0.000092.
Values sent between devices are 32-bit elements; how exact they have to be, the bound alone decides.
No kernel may reach another device: no remote copies, remote signals or barrier semaphores. Data moves between devices by JAX's collectives and lax.ppermute only.
A program may use at most 128 MiB of HBM per device.

v0:
```python
import jax
import jax.numpy as jnp
from jax import lax
from jax.experimental import pallas as pl
from jax.experimental.pallas import tpu as pltpu
from jax.sharding import PartitionSpec as P

PL = 4
LEV = 10
ROWS = 128
COLS = 256
NPL = PL * LEV
MSG = 48
CORNER = 43
LISTS = 34
HI = 17
HPAD = 18
F32 = jnp.float32
BF16 = jnp.bfloat16
GROUPS = ROWS // 8
VM = pltpu.CompilerParams(vmem_limit_bytes=56 * 1024 * 1024)


def lane_iota(shape):
    return lax.broadcasted_iota(jnp.int32, shape, len(shape) - 1)


def row_iota(shape):
    return lax.broadcasted_iota(jnp.int32, shape, len(shape) - 2)


def lookup(row, low):
    table = jnp.broadcast_to(row, low.shape)
    return jnp.take_along_axis(table, low, axis=1, mode="promise_in_bounds")


def pick_body(
    forcing, serve, south, north, slots, weights, seed, east, north_c, land,
    surf, to_east, to_west, send_a, send_b, pool,
):
    even = lax.axis_index("lat") % 2 == 0
    step = pl.program_id(0)
    steps = pl.num_programs(0)

    @pl.when(step == 0)
    def _():
        pool[:, LISTS:, :] = jnp.zeros((PL, 40 - LISTS, 128), F32)
        for g in range(4):
            ids = jnp.concatenate(
                [serve[:, 128 * (8 * g + i + 1) : 128 * (8 * g + i + 2)] for i in range(8)], axis=0
            )
            low = ids & 127
            high = ids >> 7
            acc = [jnp.zeros((8, 128), F32) for _ in range(PL)]
            for h in range(32):
                hit = high == h
                for p in range(PL):
                    acc[p] = jnp.where(hit, lookup(forcing[p, h : h + 1, :], low), acc[p])
            for p in range(PL):
                pool[p, 1 + 8 * g : 9 + 8 * g, :] = acc[p]
        for recv, place in ((south, 0), (north, LISTS - 1)):
            low = jnp.broadcast_to(recv[4:5, :].astype(jnp.int32) & 127, (8, 128))
            for p in range(PL):
                got = lookup(recv[p : p + 1, :], low)
                pool[p, place : place + 1, :] = got[0:1, :]

    block = surf.shape[1]
    lanes = lane_iota((8, 128))
    for g in range(block // 8):
        rs = slice(8 * g, 8 * g + 8)
        image = []
        for t in range(2):
            cs = slice(128 * t, 128 * t + 128)
            acc = []
            for k in range(2):
                ids = slots[k, rs, cs]
                low = ids & 127
                high = ids >> 7
                own = [jnp.zeros((8, 128), F32) for _ in range(PL)]
                for h in range(LISTS):
                    hit = high == h
                    for p in range(PL):
                        own[p] = jnp.where(hit, lookup(pool[p, h : h + 1, :], low), own[p])
                acc.append(own)
            image.append(
                [weights[0, rs, cs] * acc[0][p] + weights[1, rs, cs] * acc[1][p] for p in range(PL)]
            )
        for p in range(PL):
            surf[p, rs, 0:128] = image[0][p]
            surf[p, rs, 128:256] = image[1][p]
        pair = lanes >> 1
        statics = (east, north_c, land)
        for t, out, first in ((0, to_west, 0), (1, to_east, 126)):
            cs = slice(128 * t, 128 * t + 128)
            acc = jnp.zeros((8, 128), F32)
            for m in range(NPL + 3):
                if m < NPL:
                    p, k = divmod(m, LEV)
                    v = seed[p, k, rs, cs]
                    if k == 0:
                        v = v + image[t][p]
                else:
                    v = statics[m - NPL][rs, cs].astype(F32)
                shift = (2 * m - first) % 128
                if shift:
                    v = pltpu.roll(v, shift, 1)
                acc = jnp.where(pair == m, v, acc)
            out[rs, :] = acc

    def rows_out(out, adjacent, second):
        out[...] = jnp.zeros_like(out)
        for c, r in ((0, adjacent), (1, second)):
            for t in range(2):
                cs = slice(128 * t, 128 * t + 128)
                for m in range(NPL):
                    p, k = divmod(m, LEV)
                    v = seed[p, k, r : r + 1, cs]
                    if k == 0:
                        v = v + surf[p, r : r + 1, cs]
                    out[2 * c + t, m : m + 1, :] = v
                out[2 * c + t, 40:41, :] = east[r : r + 1, cs]
                out[2 * c + t, 41:42, :] = north_c[r : r + 1, cs]
                out[2 * c + t, 42:43, :] = land[r : r + 1, cs].astype(F32)

    for flag, low_out, high_out in ((even, send_b, send_a), (jnp.logical_not(even), send_a, send_b)):

        @pl.when(jnp.logical_and(flag, step == 0))
        def _():
            rows_out(low_out, 0, 1)

        @pl.when(jnp.logical_and(flag, step == steps - 1))
        def _():
            rows_out(high_out, block - 1, block - 2)


def pick(forcing, serve, south, north, slots, weights, seed, east, north_c, land):
    block = 16
    whole = lambda *shape: pl.BlockSpec(shape, lambda i: (0,) * len(shape))
    tile = pl.BlockSpec((block, COLS), lambda i: (i, 0))
    pair = pl.BlockSpec((2, block, COLS), lambda i: (0, i, 0))
    return pl.pallas_call(
        pick_body,
        grid=(ROWS // block,),
        in_specs=[
            whole(PL, 32, 128), whole(1, LISTS * 128), whole(8, 128), whole(8, 128), pair, pair,
            pl.BlockSpec((PL, LEV, block, COLS), lambda i: (0, 0, i, 0)), tile, tile, tile,
        ],
        out_specs=[
            pl.BlockSpec((PL, block, COLS), lambda i: (0, i, 0)),
            pl.BlockSpec((block, 128), lambda i: (i, 0)),
            pl.BlockSpec((block, 128), lambda i: (i, 0)),
            whole(4, MSG, 128),
            whole(4, MSG, 128),
        ],
        out_shape=[
            jax.ShapeDtypeStruct((PL, ROWS, COLS), F32),
            jax.ShapeDtypeStruct((ROWS, 128), F32),
            jax.ShapeDtypeStruct((ROWS, 128), F32),
            jax.ShapeDtypeStruct((4, MSG, 128), F32),
            jax.ShapeDtypeStruct((4, MSG, 128), F32),
        ],
        scratch_shapes=[pltpu.VMEM((PL, 40, 128), F32)],
        compiler_params=VM,
        name="pick",
    )(forcing, serve, south, north, slots, weights, seed, east, north_c, land)


def corner_body(west_first, west_last, east_first, east_last, tile_a, tile_b, out_a, out_b):
    even = lax.axis_index("lat") % 2 == 0
    odd = (lane_iota((8, 128)) & 1) == 1
    low = jnp.where(odd, west_first[0:1, :], east_first[0:1, :])
    high = jnp.where(odd, west_last[7:8, :], east_last[7:8, :])
    here = row_iota((8, 128)) == CORNER - 40
    out_a[0] = jnp.where(here, jnp.where(even, high, low), tile_a[0])
    out_b[0] = jnp.where(here, jnp.where(even, low, high), tile_b[0])


def corners(west, east, send_a, send_b):
    first = pl.BlockSpec((8, 128), lambda i: (0, 0))
    last = pl.BlockSpec((8, 128), lambda i: (GROUPS - 1, 0))
    spot = pl.BlockSpec((1, 8, 128), lambda i: (0, 5, 0))
    message = jax.ShapeDtypeStruct((4, MSG, 128), F32)
    return pl.pallas_call(
        corner_body,
        grid=(1,),
        in_specs=[first, last, first, last, spot, spot],
        out_specs=[spot, spot],
        out_shape=[message, message],
        input_output_aliases={4: 0, 5: 1},
        name="corners",
    )(west, west, east, east, send_a, send_b)


def ring(
    vert, to_east, to_west, west, east, send_a, send_b, got_a, got_b,
    rows_south, rows_north, rows_south1, rows_north1, west1, east1,
):
    place = lax.axis_index("lat")
    even = place % 2 == 0
    fold = place == lax.axis_size("lat") - 1
    lanes = lane_iota((1, 128))
    odd = (lanes & 1) == 1

    def chosen(flag, yes, no):
        return jnp.where(flag, yes, no)

    a = got_a[...]
    b = got_b[...]
    above = chosen(even, a, b)
    below = chosen(even, b, a)
    top = chosen(even, send_a[...], send_b[...])
    bottom = chosen(even, send_b[...], send_a[...])
    back = 127 - lane_iota((MSG, 128))
    flip = lambda x: jnp.take_along_axis(x, back, axis=1, mode="promise_in_bounds")
    turned = [flip(above[1]), flip(above[0]), flip(above[3]), flip(above[2])]
    corner_above = above[0, CORNER : CORNER + 1, :]
    corner_below = below[0, CORNER : CORNER + 1, :]
    swapped = jnp.where(odd, pltpu.roll(corner_above, 1, 1), pltpu.roll(corner_above, 127, 1))
    pick_lane = lambda x, lane: jnp.sum(jnp.where(lane_iota(x.shape) == lane, x, 0.0), axis=1, keepdims=True)
    e_above = jnp.concatenate([above[0, 40:41, :], above[1, 40:41, :]], axis=1)
    e_turn = jnp.concatenate([turned[0][40:41, :], turned[1][40:41, :]], axis=1)
    wide = lane_iota((1, COLS))
    e_edge = pick_lane(corner_above, 81)
    e_fold = jnp.where(wide == 255, e_edge, pltpu.roll(e_turn, 255, 1))
    e_fold_west = e_turn[:, 0:1]

    n0 = jnp.concatenate([chosen(fold, turned[0], above[0]), chosen(fold, turned[1], above[1])], axis=1)
    n1 = jnp.concatenate([chosen(fold, turned[2], above[2]), chosen(fold, turned[3], above[3])], axis=1)
    s0 = jnp.concatenate([below[0], below[1]], axis=1)
    s1 = jnp.concatenate([below[2], below[3]], axis=1)
    own_top = jnp.concatenate([top[0], top[1]], axis=1)
    own_bottom = jnp.concatenate([bottom[0], bottom[1]], axis=1)
    corner_n = chosen(fold, swapped, corner_above)
    e_n = chosen(fold, e_fold, e_above)
    e_n_west = chosen(fold, e_fold_west, e_edge)
    toward_n = chosen(fold, n0[41:42, :], own_top[41:42, :])
    away_n = chosen(fold, n1[41:42, :], n0[41:42, :])

    def level_coefs(plane):
        level = plane % LEV
        upper = jnp.zeros(plane.shape, F32)
        lower = jnp.zeros(plane.shape, F32)
        for k in range(LEV - 1):
            upper = jnp.where(level == k, vert[k], upper)
            lower = jnp.where(level == k + 1, vert[k], lower)
        return upper, lower

    row_up, row_down = level_coefs(row_iota((MSG, COLS)))

    def row_step(cur, toward, away, toward_c, away_c, e_row, e_west, corner):
        spread = jnp.broadcast_to(corner, (MSG, 128))
        where = lane_iota((MSG, 128))
        plane = row_iota((MSG, 128))
        from_west = jnp.sum(jnp.where(where == 2 * plane + 1, spread, 0.0), axis=1, keepdims=True)
        from_east = jnp.sum(jnp.where(where == 2 * plane, spread, 0.0), axis=1, keepdims=True)
        lane = lane_iota((MSG, COLS))
        east_u = jnp.where(lane == COLS - 1, from_east, pltpu.roll(cur, COLS - 1, 1))
        west_u = jnp.where(lane == 0, from_west, pltpu.roll(cur, 1, 1))
        e_left = jnp.where(wide == 0, e_west, pltpu.roll(e_row, 1, 1))
        up = pltpu.roll(cur, MSG - 1, 0)
        down = pltpu.roll(cur, 1, 0)
        wet = cur[42:43, :]
        return wet * (
            cur
            + e_row * (east_u - cur)
            + e_left * (west_u - cur)
            + toward_c * (toward - cur)
            + away_c * (away - cur)
            + row_up * (up - cur)
            + row_down * (down - cur)
        )

    n_first = row_step(n0, own_top, n1, toward_n, away_n, e_n, e_n_west, corner_n)
    s_first = row_step(
        s0, own_bottom, s1, s0[41:42, :], s1[41:42, :], s0[40:41, :], pick_lane(corner_below, 81), corner_below
    )
    rows_north[...] = n0
    rows_south[...] = s0
    rows_north1[...] = n_first
    rows_south1[...] = s_first

    shape = (ROWS, 128)
    lane = lane_iota(shape)
    row = row_iota(shape)
    col_up, col_down = level_coefs(lane_iota((1, 128)) >> 1)

    def col_step(cur, east_u, west_u, e_right, e_left, n_col, n_south, wet):
        north_u = jnp.where(row == ROWS - 1, corner_n, pltpu.roll(cur, ROWS - 1, 0))
        south_u = jnp.where(row == 0, corner_below, pltpu.roll(cur, 1, 0))
        n_below = jnp.where(row_iota((ROWS, 1)) == 0, n_south, pltpu.roll(jnp.broadcast_to(n_col, shape), 1, 0))
        return wet * (
            cur
            + e_right * (east_u - cur)
            + e_left * (west_u - cur)
            + n_col * (north_u - cur)
            + n_below * (south_u - cur)
            + col_up * (pltpu.roll(cur, 126, 1) - cur)
            + col_down * (pltpu.roll(cur, 2, 1) - cur)
        )

    w = west[...]
    e = east[...]
    mine_w = to_west[...]
    mine_e = to_east[...]
    lane_of = lambda x, n: x[:, n : n + 1]
    west1[...] = col_step(
        w, pltpu.roll(mine_w, 1, 1), pltpu.roll(w, 1, 1), lane_of(w, 81), lane_of(w, 80),
        lane_of(w, 83), pick_lane(corner_below, 83), lane_of(w, 85),
    )
    east1[...] = col_step(
        e, pltpu.roll(e, 127, 1), pltpu.roll(mine_e, 127, 1), lane_of(e, 80), lane_of(mine_e, 81),
        lane_of(e, 82), pick_lane(corner_below, 82), lane_of(e, 84),
    )


def step_body(
    vert, seed, surf, east, north, land, to_east, to_west, west0, east0, send_a, send_b, got_a, got_b,
    out, total, start, first, coef, side, west1, east1, south0, north0, south1, north1,
):
    p = pl.program_id(0)

    @pl.when(p == 0)
    def _():
        ring(
            vert, to_east, to_west, west0, east0, send_a, send_b, got_a, got_b,
            south0, north0, south1, north1, west1, east1,
        )

    @pl.when(p == 0)
    def _():
        wide = lane_iota((ROWS, COLS))
        tall = row_iota((ROWS, COLS))
        e = east[...]
        n = north[...]
        wet = land[...].astype(F32)
        e_left = jnp.where(wide == 0, west0[:, 81:82], pltpu.roll(e, 1, 1))
        n_below = jnp.where(tall == 0, south0[41:42, :], pltpu.roll(n, 1, 0))
        coef[0] = wet * e
        coef[1] = wet * e_left
        coef[2] = wet * n
        coef[3] = wet * n_below
        coef[4] = wet - wet * (e + e_left + n + n_below)
        coef[5] = wet

    turn = 128 - 2 * LEV * p
    odd = (lane_iota((ROWS, 128)) & 1) == 1
    for i, w, e in ((0, west0, east0), (1, west1, east1)):
        pack = pltpu.roll(jnp.where(odd, w[...], pltpu.roll(e[...], 2, 1)), turn, 1)
        for k in range(LEV):
            side[i, k] = pltpu.roll(pack, 126 - 2 * k, 1)
    for k in range(LEV):
        start[k, 7:8, :] = south0[pl.ds(p * LEV + k, 1), :]
        start[k, 136:137, :] = north0[pl.ds(p * LEV + k, 1), :]
        first[k, 7:8, :] = south1[pl.ds(p * LEV + k, 1), :]
        first[k, 136:137, :] = north1[pl.ds(p * LEV + k, 1), :]
        block = seed[0, k]
        if k == 0:
            block = block + surf[0]
        start[k, 8:136, :] = block

    lane = lane_iota((8, 128))
    sub = row_iota((8, 128))

    def advance(src, edge_at, store):
        def group(g, carry):
            row = pl.multiple_of(g * 8, 8)
            here = pl.ds(row + 8, 8)
            cs = [slice(0, 128), slice(128, 256)]
            c = [[coef[i, pl.ds(row, 8), cs[t]] for t in range(2)] for i in range(6)]
            below = [None, None]
            u = [src[0, here, cs[t]] for t in range(2)]
            for k in range(LEV):
                edge = side[edge_at, k, pl.ds(row, 8), :]
                east_of = [jnp.where(lane == 0, u[1], u[0]), jnp.where(lane == 0, edge, u[1])]
                west_of = [jnp.where(lane == 127, edge, u[0]), jnp.where(lane == 127, u[0], u[1])]
                ahead = [None, None]
                for t in range(2):
                    up_rows = src[k, pl.ds(row + 16, 8), cs[t]]
                    dn_rows = src[k, pl.ds(row, 8), cs[t]]
                    north_u = pltpu.roll(jnp.where(sub == 0, up_rows, u[t]), 7, 0)
                    south_u = pltpu.roll(jnp.where(sub == 7, dn_rows, u[t]), 1, 0)
                    east_u = pltpu.roll(east_of[t], 127, 1)
                    west_u = pltpu.roll(west_of[t], 1, 1)
                    new = (
                        c[4][t] * u[t]
                        + c[0][t] * east_u
                        + c[1][t] * west_u
                        + c[2][t] * north_u
                        + c[3][t] * south_u
                    )
                    flux = None
                    if k + 1 < LEV:
                        ahead[t] = src[k + 1, here, cs[t]]
                        flux = vert[k] * (ahead[t] - u[t])
                    if flux is None:
                        new = new - c[5][t] * below[t]
                    elif below[t] is None:
                        new = new + c[5][t] * flux
                    else:
                        new = new + c[5][t] * (flux - below[t])
                    below[t] = flux
                    store(k, row, cs[t], new)
                u = ahead
            return carry

        lax.fori_loop(0, GROUPS, group, 0, unroll=4)

    def keep(k, row, cs, new):
        first[k, pl.ds(row + 8, 8), cs] = new

    def finish(k, row, cs, new):
        out[0, k, pl.ds(row, 8), cs] = new
        if k == 0:
            total[0, pl.ds(row, 8), cs] = new + first[0, pl.ds(row + 8, 8), cs]

    advance(start, 0, keep)
    advance(first, 1, finish)


def steps(vert, seed, surf, east, north, land, to_east, to_west, west, east_in, send_a, send_b, got_a, got_b):
    whole = lambda *shape: pl.BlockSpec(shape, lambda i: (0,) * len(shape))
    tile = whole(ROWS, COLS)
    cols = whole(ROWS, 128)
    message = whole(4, MSG, 128)
    plane = pl.BlockSpec((1, ROWS, COLS), lambda i: (i, 0, 0))
    stack = pl.BlockSpec((1, LEV, ROWS, COLS), lambda i: (i, 0, 0, 0))
    return pl.pallas_call(
        step_body,
        grid=(PL,),
        in_specs=[pl.BlockSpec(memory_space=pltpu.SMEM), stack, plane, tile, tile, tile]
        + [cols] * 4
        + [message] * 4,
        out_specs=[stack, plane],
        out_shape=[
            jax.ShapeDtypeStruct((PL, LEV, ROWS, COLS), F32),
            jax.ShapeDtypeStruct((PL, ROWS, COLS), F32),
        ],
        scratch_shapes=[
            pltpu.VMEM((LEV, ROWS + 16, COLS), F32),
            pltpu.VMEM((LEV, ROWS + 16, COLS), F32),
            pltpu.VMEM((6, ROWS, COLS), F32),
            pltpu.VMEM((2, LEV, ROWS, 128), F32),
            pltpu.VMEM((ROWS, 128), F32),
            pltpu.VMEM((ROWS, 128), F32),
            pltpu.VMEM((MSG, COLS), F32),
            pltpu.VMEM((MSG, COLS), F32),
            pltpu.VMEM((MSG, COLS), F32),
            pltpu.VMEM((MSG, COLS), F32),
        ],
        compiler_params=VM,
        name="steps",
    )(vert, seed, surf, east, north, land, to_east, to_west, west, east_in, send_a, send_b, got_a, got_b)


def hot_low(ids):
    grid = row_iota((COLS, ids.shape[1]))
    return jnp.where(grid == (ids & 255), 1.0, 0.0).astype(BF16)


def hot_high(ids, parts, count):
    high = jnp.broadcast_to(ids >> 8, parts.shape)
    return jnp.concatenate([jnp.where(high == h, parts, 0.0) for h in range(count)], axis=0).astype(BF16)


def two_parts(values):
    big = values.astype(BF16).astype(F32)
    return jnp.concatenate([big, values - big], axis=0)


CONTRACT = (((1,), (1,)), ((), ()))


def spread_body(total, weights, slots, sums, to_north, to_south, grid_low):
    grid_low[...] = row_iota((COLS, COLS)).astype(F32).astype(BF16)
    which = (row_iota((16, COLS)) >> 3).astype(F32)
    pairs = HPAD // 2

    def accumulate(acc0, acc1):
        accs = (acc0, acc1)

        def block(i, carry):
            rows = pl.ds(pl.multiple_of(i * 8, 8), 8)
            ids_all = [slots[k, rows, :] for k in range(2)]
            w_all = [weights[k, rows, :] for k in range(2)]
            t_all = [total[p, rows, :] for p in range(PL)]
            unit = 0
            for r in range(8):
                surface = jnp.concatenate([t[r : r + 1, :] for t in t_all], axis=0)
                for k in range(2):
                    ids = ids_all[k][r : r + 1, :]
                    low = jnp.broadcast_to((ids & 255).astype(F32), (16, COLS)).astype(BF16)
                    low = jnp.concatenate([low] * 16, axis=0)
                    one_hot = jnp.where(grid_low[...] == low, jnp.array(1, BF16), jnp.array(0, BF16))
                    parts = two_parts(surface * w_all[k][r : r + 1, :])
                    parts = jnp.concatenate([parts, parts], axis=0).astype(BF16)
                    high = jnp.broadcast_to((ids >> 8).astype(F32), (16, COLS)) - which
                    high = high.astype(BF16)
                    hot = jnp.concatenate(
                        [jnp.where(high == jnp.array(2 * h, BF16), parts, jnp.array(0, BF16)) for h in range(pairs)],
                        axis=0,
                    )
                    m = unit % 2
                    reg = (unit // 2) % 2
                    pltpu.matmul_push_rhs(one_hot, reg, m, transpose=True)
                    pltpu.matmul_acc_lhs(accs[m], hot, load_staged_rhs=reg)
                    unit += 1
            return carry

        lax.fori_loop(0, GROUPS, block, 0)
        summed = pltpu.matmul_pop(acc0) + pltpu.matmul_pop(acc1)
        sums[...] = summed
        to_north[...] = summed[128:136, 128:] + pltpu.roll(summed[128:136, 128:], 4, 0)
        to_south[...] = summed[0:8, :128] + pltpu.roll(summed[0:8, :128], 4, 0)

    pl.run_scoped(accumulate, *[pltpu.ACC(m)((HPAD * 8, COLS), F32) for m in range(2)])


def spread(total, weights, slots):
    whole = lambda *shape: pl.BlockSpec(shape, lambda i: (0,) * len(shape))
    small = jax.ShapeDtypeStruct((8, 128), F32)
    return pl.pallas_call(
        spread_body,
        grid=(1,),
        in_specs=[whole(PL, ROWS, COLS), whole(2, ROWS, COLS), whole(2, ROWS, COLS)],
        out_specs=[whole(HPAD * 8, COLS), whole(8, 128), whole(8, 128)],
        out_shape=[jax.ShapeDtypeStruct((HPAD * 8, COLS), F32), small, small],
        scratch_shapes=[pltpu.VMEM((COLS, COLS), BF16)],
        compiler_params=VM,
        name="spread",
    )(total, weights, slots)


def gather_body(sums, south, north, serve, out):
    lane = lane_iota((PL, COLS))
    acc = jnp.zeros((128, COLS), F32)
    for h in range(HI):
        tile = sums[8 * h : 8 * h + 8, :]
        values = tile[0:4, :] + tile[4:8, :]
        if h == 0:
            values = jnp.where(lane < 128, jnp.concatenate([south[0:4, :], south[0:4, :]], axis=1), values)
        if h == HI - 1:
            values = jnp.where(lane >= 128, jnp.concatenate([north[0:4, :], north[0:4, :]], axis=1), values)
        ids = serve[:, COLS * h : COLS * h + COLS]
        acc = acc + lax.dot_general(
            hot_high(ids, two_parts(values), 16), hot_low(ids), CONTRACT, preferred_element_type=F32
        )
    for h in range(16):
        tile = acc[8 * h : 8 * h + 8, :]
        values = tile[0:4, :] + tile[4:8, :]
        for p in range(PL):
            for t in range(2):
                out[p, 2 * h + t : 2 * h + t + 1, :] = values[p : p + 1, 128 * t : 128 * t + 128]


def gather(sums, south, north, serve):
    whole = lambda *shape: pl.BlockSpec(shape, lambda i: (0,) * len(shape))
    return pl.pallas_call(
        gather_body,
        grid=(1,),
        in_specs=[whole(HPAD * 8, COLS), whole(8, 128), whole(8, 128), whole(1, LISTS * 128)],
        out_specs=whole(PL, 32, 128),
        out_shape=jax.ShapeDtypeStruct((PL, 32, 128), F32),
        compiler_params=VM,
        name="gather",
    )(sums, south, north, serve)


def ladder(lon_count, lat_count, shift):
    place = lambda a, j: j * lat_count + a
    pairs = []
    for j in range(lon_count):
        for a in range(1, lat_count - 1, 2):
            pairs.append((place(a, j), place(a + 1, j)))
            pairs.append((place(a + 1, j), place(a, j)))
        pairs.append((place(lat_count - 1, j), place(lat_count - 1, (shift - 1 - j) % lon_count)))
    return pairs


def shards(
    ocean_seed, forcing_pert, land_mask, east_coef, north_coef, vert_coef, remap_weight, ocean_slots,
    serve_cells, fold_map,
):
    lat_count = lax.axis_size("lat")
    lon_count = lax.axis_size("lon")
    upward = [(i, i + 1) for i in range(lat_count - 1)]
    downward = [(i + 1, i) for i in range(lat_count - 1)]
    eastward = [(i, (i + 1) % lon_count) for i in range(lon_count)]
    westward = [((i + 1) % lon_count, i) for i in range(lon_count)]

    cells = serve_cells.reshape(-1)

    def list_message(row, ids):
        return jnp.concatenate([row, ids.astype(F32)[None], jnp.zeros((3, 128), F32)], axis=0)

    south_list = lax.ppermute(list_message(forcing_pert[:, -1], cells[-128:]), "lat", upward)
    north_list = lax.ppermute(list_message(forcing_pert[:, 0], cells[:128]), "lat", downward)

    surf, to_east, to_west, send_a, send_b = pick(
        forcing_pert, serve_cells, south_list, north_list, ocean_slots, remap_weight,
        ocean_seed, east_coef, north_coef, land_mask,
    )

    west = lax.ppermute(to_east, "lon", eastward)
    east = lax.ppermute(to_west, "lon", westward)
    send_a, send_b = corners(west, east, send_a, send_b)
    shift = ((fold_map[0] + 1) // COLS) % lon_count
    got_a = lax.ppermute(send_a, "lat", [(i ^ 1, i) for i in range(lat_count)])
    got_b = lax.switch(
        shift,
        [
            lambda v, s=s: lax.ppermute(v, ("lon", "lat"), ladder(lon_count, lat_count, s))
            for s in range(lon_count)
        ],
        send_b,
    )
    adjoint_two, total = steps(
        vert_coef, ocean_seed, surf, east_coef, north_coef, land_mask, to_east, to_west, west, east,
        send_a, send_b, got_a, got_b,
    )
    sums, to_north, to_south = spread(total, remap_weight, ocean_slots)
    from_south = lax.ppermute(to_north, "lat", upward)
    from_north = lax.ppermute(to_south, "lat", downward)
    stress_sens = gather(sums, from_south, from_north, serve_cells)
    return (adjoint_two, stress_sens)


def solution(mesh):
    return jax.shard_map(
        shards,
        mesh=mesh,
        in_specs=(
            P(None, None, "lat", "lon"),
            P(None, "lat", "lon"),
            P("lat", "lon"),
            P("lat", "lon"),
            P("lat", "lon"),
            P(),
            P(None, "lat", "lon"),
            P(None, "lat", "lon"),
            P("lat", "lon"),
            P(),
        ),
        out_specs=(P(None, None, "lat", "lon"), P(None, "lat", "lon")),
        check_vma=False,
    )
```

profile of v0, /device:TPU:24, one launch (start us, length us, event | category | flops | bytes accessed | tf_op | source)
XLA Modules:
  0.0 98.5 jit_solution(2805227151265980488)
XLA Ops:
  0.6 0.7 slice_convert_fusion
  1.3 0.7 fusion
  2.0 0.1 pad.5.clone
  2.1 0.1 maximum_maximum_fusion.1
  2.2 2.6 %collective-permute-start.17 = (f32[8,128]{1,0:T(8,128)S(1)}, f32[8,128]{1,0:T(8,128)S(1)}, u32[]{:S(2)}, u32[]{:S(2)}) collective-permute-start(f32[8,128]{1,0:T(8,128)S(1)} %get-tuple-element.63), channel_id=1, source_target_pairs={{1,0},{2,1},{3,2},{4,3},{5,4},{6,5},{7,6},{9,8},{10,9},{11,10},{12... | collective-permute-start | bytes 12296 | tf_op jit(solution)/shard_map/ppermute | solution.py:596
  4.8 6.8 %collective-permute-start.16 = (f32[8,128]{1,0:T(8,128)S(1)}, f32[8,128]{1,0:T(8,128)S(1)}, u32[]{:S(2)}, u32[]{:S(2)}) collective-permute-start(f32[8,128]{1,0:T(8,128)S(1)} %get-tuple-element.64), channel_id=1, source_target_pairs={{0,1},{1,2},{2,3},{3,4},{4,5},{5,6},{6,7},{8,9},{9,10},{10,11},{11... | collective-permute-start | bytes 12296 | tf_op jit(solution)/shard_map/ppermute | solution.py:595
  11.7 0.0 collective-permute-done.17.north
  11.7 0.0 copy-start.5
  11.7 1.3 %collective-permute-done.16.south = f32[8,128]{1,0:T(8,128)S(1)} collective-permute-done((f32[8,128]{1,0:T(8,128)S(1)}, f32[8,128]{1,0:T(8,128)S(1)}, u32[]{:S(2)}, u32[]{:S(2)}) %collective-permute-start.16) | collective-permute-done | bytes 4128 | tf_op jit(solution)/shard_map/ppermute | solution.py:595
  13.0 0.0 copy-done.5
  13.0 0.0 copy-start.6
  13.0 0.6 copy-done.6
  13.6 15.3 %pick.1 = (f32[4,128,256]{2,1,0:T(8,128)}, f32[128,128]{1,0:T(8,128)}, f32[128,128]{1,0:T(8,128)}, f32[4,48,128]{2,1,0:T(8,128)}, f32[4,48,128]{2,1,0:T(8,128)S(1)}) custom-call(f32[4,32,128]{2,1,0:T(8,128)} %forcing.1, s32[1,4352]{1,0:T(1,128)} %serve.3, f32[8,128]{1,0:T(8,128)} %copy-done.6, f32[8,128]{1,0:T(8,128)} %copy-done.5, s32[2,128,256]{2,1,0:T(8,128)} %slots.3, ...), custom_call_target="tpu_custom_call" | custom-call | tf_op jit(solution)/shard_map/pick/pallas_call | solution.py:141
  28.9 0.1 collective-permute-start.18
  29.0 3.8 %collective-permute-start.19 = (f32[128,128]{1,0:T(8,128)}, f32[128,128]{1,0:T(8,128)S(1)}, u32[]{:S(2)}, u32[]{:S(2)}) collective-permute-start(f32[128,128]{1,0:T(8,128)} %get-tuple-element.49.to_west), channel_id=1, source_target_pairs={{8,0},{16,8},{24,16},{32,24},{40,32},{48,40},{56,48},{64,56},{72,6... | collective-permute-start | bytes 196616 | tf_op jit(solution)/shard_map/ppermute | solution.py:604
  32.8 2.2 %collective-permute-done.18.west_first.west_last.west0 = f32[128,128]{1,0:T(8,128)S(1)} collective-permute-done((f32[128,128]{1,0:T(8,128)}, f32[128,128]{1,0:T(8,128)S(1)}, u32[]{:S(2)}, u32[]{:S(2)}) %collective-permute-start.18) | collective-permute-done | bytes 65568 | tf_op jit(solution)/shard_map/ppermute | solution.py:603
  35.0 0.0 copy-start
  35.0 0.1 collective-permute-done.19.east_first.east_last.east0
  35.0 0.0 copy-start.1
  35.0 0.6 copy-done
  35.6 0.1 copy-done.1
  35.6 1.3 %corners.1 = (f32[4,48,128]{2,1,0:T(8,128)}, f32[4,48,128]{2,1,0:T(8,128)S(1)}) custom-call(f32[128,128]{1,0:T(8,128)} %copy-done, f32[128,128]{1,0:T(8,128)} %copy-done, f32[128,128]{1,0:T(8,128)} %copy-done.1, f32[128,128]{1,0:T(8,128)} %copy-done.1, f32[4,48,128]{2,1,0:T(8,128)} %get-tuple-element.50.tile_a, ...), custom_call_target="tpu_custom_call", output_to_operand_aliasing={{0}: (4, {}), {1}: (5, {})} | custom-call | tf_op jit(solution)/shard_map/corners/pallas_call | solution.py:183
  37.0 0.0 collective-permute-start.20
  37.0 1.2 %slice.21 = s32[1]{0:T(128)} slice(s32[4096]{0:T(1024)} %param.35), slice={[0:1]} | slice | bytes 8 | tf_op jit(solution)/shard_map/slice | solution.py:606
  38.9 10.9 %conditional.1 = (f32[4,48,128]{2,1,0:T(8,128)}) conditional(s32[]{:T(128)} %clamp.3, f32[4,48,128]{2,1,0:T(8,128)S(1)} %get-tuple-element.53.send_b, f32[4,48,128]{2,1,0:T(8,128)S(1)} %get-tuple-element.53.send_b, f32[4,48,128]{2,1,0:T(8,128)S(1)} %get-tuple-element.53.send_b, ...), branch_computations={%region_0.1_spmd, %region_1.2_spmd, %region_2.3_spmd, %region_3.4_... | conditional | bytes 393264 | solution.py:608
  38.9 7.8 %collective-permute-start.11 = (f32[4,48,128]{2,1,0:T(8,128)S(1)}, f32[4,48,128]{2,1,0:T(8,128)}, u32[]{:S(2)}, u32[]{:S(2)}) collective-permute-start(f32[4,48,128]{2,1,0:T(8,128)S(1)} %param.11), channel_id=1, source_target_pairs={{1,2},{2,1},{3,4},{4,3},{5,6},{6,5},{7,87},{9,10},{10,9},{11,12},{... | collective-permute-start | bytes 294920 | tf_op jit(solution)/shard_map/cond/branch_11_fun/ppermute | solution.py:611
  46.7 3.1 %collective-permute-done.11 = f32[4,48,128]{2,1,0:T(8,128)} collective-permute-done((f32[4,48,128]{2,1,0:T(8,128)S(1)}, f32[4,48,128]{2,1,0:T(8,128)}, u32[]{:S(2)}, u32[]{:S(2)}) %collective-permute-start.11) | collective-permute-done | bytes 98336 | tf_op jit(solution)/shard_map/cond/branch_11_fun/ppermute | solution.py:611
  49.8 0.0 collective-permute-done.20.got_a
  49.8 0.0 copy-start.2
  49.8 0.6 copy-done.2
  50.4 15.2 %steps.1 = (f32[4,10,128,256]{3,2,1,0:T(8,128)}, f32[4,128,256]{2,1,0:T(8,128)}) custom-call(f32[9]{0:T(128)} %vert.1, f32[4,10,128,256]{3,2,1,0:T(8,128)} %seed.3, f32[4,128,256]{2,1,0:T(8,128)} %get-tuple-element.47.surf, f32[128,256]{1,0:T(8,128)} %east.3, f32[128,256]{1,0:T(8,128)} %north.1, s32[128,256]{1,0:T(8,128)} %land.3, ...), custom_call_target="tpu_custom_call" | custom-call | tf_op jit(solution)/shard_map/steps/pallas_call | solution.py:427
  65.6 13.2 %spread.1 = (f32[144,256]{1,0:T(8,128)}, f32[8,128]{1,0:T(8,128)}, f32[8,128]{1,0:T(8,128)}) custom-call(f32[4,128,256]{2,1,0:T(8,128)} %get-tuple-element.55.total, f32[2,128,256]{2,1,0:T(8,128)} %weights.3, s32[2,128,256]{2,1,0:T(8,128)} %slots.3), custom_call_target="tpu_custom_call" | custom-call | tf_op jit(solution)/shard_map/spread/pallas_call | solution.py:521
  78.8 7.2 %collective-permute-start.21 = (f32[8,128]{1,0:T(8,128)}, f32[8,128]{1,0:T(8,128)S(1)}, u32[]{:S(2)}, u32[]{:S(2)}) collective-permute-start(f32[8,128]{1,0:T(8,128)} %get-tuple-element.57), channel_id=1, source_target_pairs={{0,1},{1,2},{2,3},{3,4},{4,5},{5,6},{6,7},{8,9},{9,10},{10,11},{11... | collective-permute-start | bytes 12296 | tf_op jit(solution)/shard_map/ppermute | solution.py:621
  86.1 1.9 %collective-permute-start.22 = (f32[8,128]{1,0:T(8,128)}, f32[8,128]{1,0:T(8,128)S(1)}, u32[]{:S(2)}, u32[]{:S(2)}) collective-permute-start(f32[8,128]{1,0:T(8,128)} %get-tuple-element.58), channel_id=1, source_target_pairs={{1,0},{2,1},{3,2},{4,3},{5,4},{6,5},{7,6},{9,8},{10,9},{11,10},{12... | collective-permute-start | bytes 12296 | tf_op jit(solution)/shard_map/ppermute | solution.py:622
  88.0 0.0 collective-permute-done.21.south
  88.0 0.0 copy-start.3
  88.0 7.4 %collective-permute-done.22.north = f32[8,128]{1,0:T(8,128)S(1)} collective-permute-done((f32[8,128]{1,0:T(8,128)}, f32[8,128]{1,0:T(8,128)S(1)}, u32[]{:S(2)}, u32[]{:S(2)}) %collective-permute-start.22) | collective-permute-done | bytes 4128 | tf_op jit(solution)/shard_map/ppermute | solution.py:622
  95.4 0.0 copy-start.4
  95.4 0.0 copy-done.3
  95.4 0.6 copy-done.4
  96.0 2.5 %gather.1 = f32[4,32,128]{2,1,0:T(8,128)} custom-call(f32[144,256]{1,0:T(8,128)} %get-tuple-element.56.sums, f32[8,128]{1,0:T(8,128)} %copy-done.3, f32[8,128]{1,0:T(8,128)} %copy-done.4, s32[1,4352]{1,0:T(1,128)} %serve.3), custom_call_target="tpu_custom_call" | custom-call | tf_op jit(solution)/shard_map/gather/pallas_call | solution.py:557
  (1 shorter events, 0.0 us)
Async XLA Ops:
  2.2 9.5 %collective-permute-start.17 = (f32[8,128]{1,0:T(8,128)S(1)}, f32[8,128]{1,0:T(8,128)S(1)}, u32[]{:S(2)}, u32[]{:S(2)}) collective-permute-start(f32[8,128]{1,0:T(8,128)S(1)} %get-tuple-element.63), channel_id=1, source_target_pairs={{1,0},{2,1},{3,2},{4,3},{5,4},{6,5},{7,6},{9,8},{10,9},{11,10},{12... | collective-permute-start | bytes 12296 | tf_op jit(solution)/shard_map/ppermute | solution.py:596
  4.8 8.1 %collective-permute-start.16 = (f32[8,128]{1,0:T(8,128)S(1)}, f32[8,128]{1,0:T(8,128)S(1)}, u32[]{:S(2)}, u32[]{:S(2)}) collective-permute-start(f32[8,128]{1,0:T(8,128)S(1)} %get-tuple-element.64), channel_id=1, source_target_pairs={{0,1},{1,2},{2,3},{3,4},{4,5},{5,6},{6,7},{8,9},{9,10},{10,11},{11... | collective-permute-start | bytes 12296 | tf_op jit(solution)/shard_map/ppermute | solution.py:595
  11.7 1.3 %copy-start.5 = (f32[8,128]{1,0:T(8,128)}, f32[8,128]{1,0:T(8,128)S(1)}, u32[]{:S(2)}) copy-start(f32[8,128]{1,0:T(8,128)S(1)} %collective-permute-done.17.north) | copy-start | bytes 12292
  13.0 0.6 copy-start.6
  28.9 6.1 %collective-permute-start.18 = (f32[128,128]{1,0:T(8,128)}, f32[128,128]{1,0:T(8,128)S(1)}, u32[]{:S(2)}, u32[]{:S(2)}) collective-permute-start(f32[128,128]{1,0:T(8,128)} %get-tuple-element.48.to_east), channel_id=1, source_target_pairs={{0,8},{8,16},{16,24},{24,32},{32,40},{40,48},{48,56},{56,64},{64,7... | collective-permute-start | bytes 196616 | tf_op jit(solution)/shard_map/ppermute | solution.py:603
  29.0 6.1 %collective-permute-start.19 = (f32[128,128]{1,0:T(8,128)}, f32[128,128]{1,0:T(8,128)S(1)}, u32[]{:S(2)}, u32[]{:S(2)}) collective-permute-start(f32[128,128]{1,0:T(8,128)} %get-tuple-element.49.to_west), channel_id=1, source_target_pairs={{8,0},{16,8},{24,16},{32,24},{40,32},{48,40},{56,48},{64,56},{72,6... | collective-permute-start | bytes 196616 | tf_op jit(solution)/shard_map/ppermute | solution.py:604
  35.0 0.6 copy-start
  35.0 0.6 copy-start.1
  37.0 12.8 %collective-permute-start.20 = (f32[4,48,128]{2,1,0:T(8,128)}, f32[4,48,128]{2,1,0:T(8,128)S(1)}, u32[]{:S(2)}, u32[]{:S(2)}) collective-permute-start(f32[4,48,128]{2,1,0:T(8,128)} %get-tuple-element.52.send_a), channel_id=1, source_target_pairs={{1,0},{0,1},{3,2},{2,3},{5,4},{4,5},{7,6},{6,7},{9,8},{8,9},{11,10... | collective-permute-start | bytes 294920 | tf_op jit(solution)/shard_map/ppermute | solution.py:607
  38.9 10.9 %collective-permute-start.11 = (f32[4,48,128]{2,1,0:T(8,128)S(1)}, f32[4,48,128]{2,1,0:T(8,128)}, u32[]{:S(2)}, u32[]{:S(2)}) collective-permute-start(f32[4,48,128]{2,1,0:T(8,128)S(1)} %param.11), channel_id=1, source_target_pairs={{1,2},{2,1},{3,4},{4,3},{5,6},{6,5},{7,87},{9,10},{10,9},{11,12},{... | collective-permute-start | bytes 294920 | tf_op jit(solution)/shard_map/cond/branch_11_fun/ppermute | solution.py:611
  49.8 0.6 copy-start.2
  78.8 9.2 %collective-permute-start.21 = (f32[8,128]{1,0:T(8,128)}, f32[8,128]{1,0:T(8,128)S(1)}, u32[]{:S(2)}, u32[]{:S(2)}) collective-permute-start(f32[8,128]{1,0:T(8,128)} %get-tuple-element.57), channel_id=1, source_target_pairs={{0,1},{1,2},{2,3},{3,4},{4,5},{5,6},{6,7},{8,9},{9,10},{10,11},{11... | collective-permute-start | bytes 12296 | tf_op jit(solution)/shard_map/ppermute | solution.py:621
  86.1 9.3 %collective-permute-start.22 = (f32[8,128]{1,0:T(8,128)}, f32[8,128]{1,0:T(8,128)S(1)}, u32[]{:S(2)}, u32[]{:S(2)}) collective-permute-start(f32[8,128]{1,0:T(8,128)} %get-tuple-element.58), channel_id=1, source_target_pairs={{1,0},{2,1},{3,2},{4,3},{5,4},{6,5},{7,6},{9,8},{10,9},{11,10},{12... | collective-permute-start | bytes 12296 | tf_op jit(solution)/shard_map/ppermute | solution.py:622
  88.0 7.4 %copy-start.3 = (f32[8,128]{1,0:T(8,128)}, f32[8,128]{1,0:T(8,128)S(1)}, u32[]{:S(2)}) copy-start(f32[8,128]{1,0:T(8,128)S(1)} %collective-permute-done.21.south) | copy-start | bytes 12292
  95.4 0.6 copy-start.4
where the time goes:
time: 98.9 us; the launch traced here: 98.5 us
  Pallas kernels  47.5 us (48%)
  starting transfers between devices  30.3 us (31%)
  waiting for transfers between devices  14 us (14%)
  local copies, waits for them, and re-layouts  4.45 us (4%)
  between operations  1.41 us (1%)
    pallas_call x1, Pallas kernels, pick(): pl.pallas_call(pick_body, grid=(ROWS // block,), in_specs=[whole(PL, 32,...  15.3 us
    pallas_call x1, Pallas kernels, steps(): pl.pallas_call(step_body, grid=(PL,), in_specs=[pl.BlockSpec(memory_space...  15.2 us
    pallas_call x1, Pallas kernels, spread(): pl.pallas_call(spread_body, grid=(1,), in_specs=[whole(PL, ROWS, COLS), w...  13.2 us
    ppermute x1, starting transfers between devices, shards(): lax.ppermute(v, ('lon', 'lat'), ladder(lon_count, lat_count, s))  7.78 us
    ppermute x1, waiting for transfers between devices, shards(): from_north = lax.ppermute(to_south, 'lat', downward)  7.38 us
    ppermute x1, starting transfers between devices, shards(): from_south = lax.ppermute(to_north, 'lat', upward)  7.24 us
    ppermute x1, starting transfers between devices, shards(): lax.ppermute(list_message(forcing_pert[:, -1], cells[-128:]), 'lat', upward)  6.8 us
    ppermute x1, starting transfers between devices, shards(): east = lax.ppermute(to_west, 'lon', westward)  3.84 us
  transfers between devices with their start and end apart: 8, of which 5 were waited for; matrix products, arithmetic and copies ran while one was open for 1% of the time, Pallas kernels for 0%

commit v1 on v0

--- a/solution.py
+++ b/solution.py
@@ -313,221 +313,287 @@
     )
 
 
-def step_body(
+def hot_low(ids):
+    grid = row_iota((COLS, ids.shape[1]))
+    return jnp.where(grid == (ids & 255), 1.0, 0.0).astype(BF16)
+
+
+def hot_high(ids, parts, count):
+    high = jnp.broadcast_to(ids >> 8, parts.shape)
+    return jnp.concatenate([jnp.where(high == h, parts, 0.0) for h in range(count)], axis=0).astype(BF16)
+
+
+def two_parts(values):
+    big = values.astype(BF16).astype(F32)
+    return jnp.concatenate([big, values - big], axis=0)
+
+
+CONTRACT = (((1,), (1,)), ((), ()))
+
+
+def sweep_body(
     vert, seed, surf, east, north, land, to_east, to_west, west0, east0, send_a, send_b, got_a, got_b,
-    out, total, start, first, coef, side, west1, east1, south0, north0, south1, north1,
+    weights, slots,
+    out, sums, to_north, to_south,
+    start0, start1, start2, start3, first0, first1, first2, first3, result, total, coef, side,
+    west1, east1, south0, north0, south1, north1, grid_low, arrive, leave,
 ):
-    p = pl.program_id(0)
-
-    @pl.when(p == 0)
-    def _():
-        ring(
-            vert, to_east, to_west, west0, east0, send_a, send_b, got_a, got_b,
-            south0, north0, south1, north1, west1, east1,
+    start = (start0, start1, start2, start3)
+    first = (first0, first1, first2, first3)
+
+    def incoming(p, g):
+        row = pl.multiple_of(g * 8, 8)
+        return pltpu.make_async_copy(
+            seed.at[p, :, pl.ds(row, 8), :], start[p].at[:, pl.ds(row + 8, 8), :], arrive.at[p, g]
         )
 
-    @pl.when(p == 0)
-    def _():
-        wide = lane_iota((ROWS, COLS))
-        tall = row_iota((ROWS, COLS))
-        e = east[...]
-        n = north[...]
-        wet = land[...].astype(F32)
-        e_left = jnp.where(wide == 0, west0[:, 81:82], pltpu.roll(e, 1, 1))
-        n_below = jnp.where(tall == 0, south0[41:42, :], pltpu.roll(n, 1, 0))
-        coef[0] = wet * e
-        coef[1] = wet * e_left
-        coef[2] = wet * n
-        coef[3] = wet * n_below
-        coef[4] = wet - wet * (e + e_left + n + n_below)
-        coef[5] = wet
-
-    turn = 128 - 2 * LEV * p
+    def outgoing(g):
+        rows = pl.ds(pl.multiple_of(g * 8, 8), 8)
+        return pltpu.make_async_copy(result.at[:, :, rows, :], out.at[:, :, rows, :], leave.at[g])
+
+    def fetch(g, carry):
+        for p in range(PL):
+            incoming(p, g).start()
+        return carry
+
+    lax.fori_loop(0, GROUPS, fetch, 0)
+
+    ring(
+        vert, to_east, to_west, west0, east0, send_a, send_b, got_a, got_b,
+        south0, north0, south1, north1, west1, east1,
+    )
+    wide = lane_iota((ROWS, COLS))
+    tall = row_iota((ROWS, COLS))
+    e = east[...]
+    n = north[...]
+    wet = land[...].astype(F32)
+    e_left = jnp.where(wide == 0, west0[:, 81:82], pltpu.roll(e, 1, 1))
+    n_below = jnp.where(tall == 0, south0[41:42, :], pltpu.roll(n, 1, 0))
+    coef[0] = wet * e
+    coef[1] = wet * e_left
+    coef[2] = wet * n
+    coef[3] = wet * n_below
+    coef[4] = wet - wet * (e + e_left + n + n_below)
+    coef[5] = wet
     odd = (lane_iota((ROWS, 128)) & 1) == 1
-    for i, w, e in ((0, west0, east0), (1, west1, east1)):
-        pack = pltpu.roll(jnp.where(odd, w[...], pltpu.roll(e[...], 2, 1)), turn, 1)
+    for i, w, x in ((0, west0, east0), (1, west1, east1)):
+        pack = jnp.where(odd, w[...], pltpu.roll(x[...], 2, 1))
+        for p in range(PL):
+            for k in range(LEV):
+                side[i, p, k] = pltpu.roll(pack, (126 - 2 * k - 2 * LEV * p) % 128, 1)
+    for p in range(PL):
         for k in range(LEV):
-            side[i, k] = pltpu.roll(pack, 126 - 2 * k, 1)
-    for k in range(LEV):
-        start[k, 7:8, :] = south0[pl.ds(p * LEV + k, 1), :]
-        start[k, 136:137, :] = north0[pl.ds(p * LEV + k, 1), :]
-        first[k, 7:8, :] = south1[pl.ds(p * LEV + k, 1), :]
-        first[k, 136:137, :] = north1[pl.ds(p * LEV + k, 1), :]
-        block = seed[0, k]
-        if k == 0:
-            block = block + surf[0]
-        start[k, 8:136, :] = block
-
+            m = p * LEV + k
+            start[p][k, 7:8, :] = south0[m : m + 1, :]
+            start[p][k, 136:137, :] = north0[m : m + 1, :]
+            first[p][k, 7:8, :] = south1[m : m + 1, :]
+            first[p][k, 136:137, :] = north1[m : m + 1, :]
+    grid_low[...] = row_iota((COLS, COLS)).astype(F32).astype(BF16)
+    which = (row_iota((16, COLS)) >> 3).astype(F32)
     lane = lane_iota((8, 128))
     sub = row_iota((8, 128))
-
-    def advance(src, edge_at, store):
-        def group(g, carry):
-            row = pl.multiple_of(g * 8, 8)
+    cs = (slice(0, 128), slice(128, 256))
+
+    def ready(g):
+        row = pl.multiple_of(g * 8, 8)
+        for p in range(PL):
+            incoming(p, g).wait()
+        for p in range(PL):
             here = pl.ds(row + 8, 8)
-            cs = [slice(0, 128), slice(128, 256)]
-            c = [[coef[i, pl.ds(row, 8), cs[t]] for t in range(2)] for i in range(6)]
-            below = [None, None]
-            u = [src[0, here, cs[t]] for t in range(2)]
-            for k in range(LEV):
-                edge = side[edge_at, k, pl.ds(row, 8), :]
-                east_of = [jnp.where(lane == 0, u[1], u[0]), jnp.where(lane == 0, edge, u[1])]
-                west_of = [jnp.where(lane == 127, edge, u[0]), jnp.where(lane == 127, u[0], u[1])]
-                ahead = [None, None]
-                for t in range(2):
-                    up_rows = src[k, pl.ds(row + 16, 8), cs[t]]
-                    dn_rows = src[k, pl.ds(row, 8), cs[t]]
-                    north_u = pltpu.roll(jnp.where(sub == 0, up_rows, u[t]), 7, 0)
-                    south_u = pltpu.roll(jnp.where(sub == 7, dn_rows, u[t]), 1, 0)
-                    east_u = pltpu.roll(east_of[t], 127, 1)
-                    west_u = pltpu.roll(west_of[t], 1, 1)
-                    new = (
-                        c[4][t] * u[t]
-                        + c[0][t] * east_u
-                        + c[1][t] * west_u
-                        + c[2][t] * north_u
-                        + c[3][t] * south_u
-                    )
-                    flux = None
-                    if k + 1 < LEV:
-                        ahead[t] = src[k + 1, here, cs[t]]
-                        flux = vert[k] * (ahead[t] - u[t])
-                    if flux is None:
-                        new = new - c[5][t] * below[t]
-                    elif below[t] is None:
-                        new = new + c[5][t] * flux
-                    else:
-                        new = new + c[5][t] * (flux - below[t])
-                    below[t] = flux
-                    store(k, row, cs[t], new)
-                u = ahead
+            start[p][0, here, :] = start[p][0, here, :] + surf[p, pl.ds(row, 8), :]
+
+    def stencil(p, g, src, at, c, store):
+        row = pl.multiple_of(g * 8, 8)
+        here = pl.ds(row + 8, 8)
+        below = [None, None]
+        u = [src[0, here, cs[t]] for t in range(2)]
+        for k in range(LEV):
+            edge = side[at, p, k, pl.ds(row, 8), :]
+            east_of = [jnp.where(lane == 0, u[1], u[0]), jnp.where(lane == 0, edge, u[1])]
+            west_of = [jnp.where(lane == 127, edge, u[0]), jnp.where(lane == 127, u[0], u[1])]
+            ahead = [None, None]
+            for t in range(2):
+                up_rows = src[k, pl.ds(row + 16, 8), cs[t]]
+                dn_rows = src[k, pl.ds(row, 8), cs[t]]
+                north_u = pltpu.roll(jnp.where(sub == 0, up_rows, u[t]), 7, 0)
+                south_u = pltpu.roll(jnp.where(sub == 7, dn_rows, u[t]), 1, 0)
+                east_u = pltpu.roll(east_of[t], 127, 1)
+                west_u = pltpu.roll(west_of[t], 1, 1)
+                new = (
+                    c[4][t] * u[t]
+                    + c[0][t] * east_u
+                    + c[1][t] * west_u
+                    + c[2][t] * north_u
+                    + c[3][t] * south_u
+                )
+                flux = None
+                if k + 1 < LEV:
+                    ahead[t] = src[k + 1, here, cs[t]]
+                    flux = vert[k] * (ahead[t] - u[t])
+                if flux is None:
+                    new = new - c[5][t] * below[t]
+                elif below[t] is None:
+                    new = new + c[5][t] * flux
+                else:
+                    new = new + c[5][t] * (flux - below[t])
+                below[t] = flux
+                store(k, row, t, new)
+            u = ahead
+
+    def coefs(g):
+        row = pl.multiple_of(g * 8, 8)
+        return [[coef[i, pl.ds(row, 8), cs[t]] for t in range(2)] for i in range(6)]
+
+    def step_one(p, g, c):
+        def keep(k, row, t, new):
+            first[p][k, pl.ds(row + 8, 8), cs[t]] = new
+
+        stencil(p, g, start[p], 0, c, keep)
+
+    def step_two(p, g, c):
+        def finish(k, row, t, new):
+            result[p, k, pl.ds(row, 8), cs[t]] = new
+            if k == 0:
+                total[p, pl.ds(row, 8), cs[t]] = new + first[p][0, pl.ds(row + 8, 8), cs[t]]
+
+        stencil(p, g, first[p], 1, c, finish)
+
+    def surfaces(g):
+        rows = pl.ds(pl.multiple_of(g * 8, 8), 8)
+        return (
+            [slots[k, rows, :] for k in range(2)],
+            [weights[k, rows, :] for k in range(2)],
+            [total[p, rows, :] for p in range(PL)],
+        )
+
+    def slot_sums(accs, loaded, lines):
+        ids_all, w_all, t_all = loaded
+        for r in lines:
+            surface = jnp.concatenate([t[r : r + 1, :] for t in t_all], axis=0)
+            for k in range(2):
+                ids = ids_all[k][r : r + 1, :]
+                low = jnp.broadcast_to((ids & 255).astype(F32), (16, COLS)).astype(BF16)
+                low = jnp.concatenate([low] * 16, axis=0)
+                one_hot = jnp.where(grid_low[...] == low, jnp.array(1, BF16), jnp.array(0, BF16))
+                parts = two_parts(surface * w_all[k][r : r + 1, :])
+                parts = jnp.concatenate([parts, parts], axis=0).astype(BF16)
+                high = (jnp.broadcast_to((ids >> 8).astype(F32), (16, COLS)) - which).astype(BF16)
+                hot = jnp.concatenate(
+                    [
+                        jnp.where(high == jnp.array(2 * h, BF16), parts, jnp.array(0, BF16))
+                        for h in range(HPAD // 2)
+                    ],
+                    axis=0,
+                )
+                pltpu.matmul_push_rhs(one_hot, r % 2, k, transpose=True)
+                pltpu.matmul_acc_lhs(accs[k], hot, load_staged_rhs=r % 2)
+
+    def accumulate(*accs):
+        ready(0)
+        ready(1)
+
+        def lead(g, carry):
+            c = coefs(g)
+            ready(g + 2)
+            for p in range(PL):
+                step_one(p, g, c)
             return carry
 
-        lax.fori_loop(0, GROUPS, group, 0, unroll=4)
-
-    def keep(k, row, cs, new):
-        first[k, pl.ds(row + 8, 8), cs] = new
-
-    def finish(k, row, cs, new):
-        out[0, k, pl.ds(row, 8), cs] = new
-        if k == 0:
-            total[0, pl.ds(row, 8), cs] = new + first[0, pl.ds(row + 8, 8), cs]
-
-    advance(start, 0, keep)
-    advance(first, 1, finish)
-
-
-def steps(vert, seed, surf, east, north, land, to_east, to_west, west, east_in, send_a, send_b, got_a, got_b):
+        lax.fori_loop(0, 2, lead, 0)
+        ready(4)
+        c = coefs(0)
+        for p in range(PL):
+            step_two(p, 0, c)
+        c = coefs(2)
+        for p in range(PL):
+            step_one(p, 2, c)
+        outgoing(0).start()
+
+        def body(i, carry):
+            @pl.when(i < GROUPS - 2)
+            def _():
+                ready(i + 2)
+
+            loaded = surfaces(i - 3)
+            c_two = coefs(i - 2)
+            c_one = coefs(i)
+            for p in range(PL):
+                slot_sums(accs, loaded, (2 * p, 2 * p + 1))
+                step_two(p, i - 2, c_two)
+                step_one(p, i, c_one)
+            outgoing(i - 2).start()
+            return carry
+
+        lax.fori_loop(3, GROUPS, body, 0)
+
+        def trail(g, carry):
+            loaded = surfaces(g - 1)
+            c = coefs(g)
+            for p in range(PL):
+                slot_sums(accs, loaded, (2 * p, 2 * p + 1))
+                step_two(p, g, c)
+            outgoing(g).start()
+            return carry
+
+        lax.fori_loop(GROUPS - 2, GROUPS, trail, 0)
+        slot_sums(accs, surfaces(GROUPS - 1), range(8))
+        summed = pltpu.matmul_pop(accs[0]) + pltpu.matmul_pop(accs[1])
+        sums[...] = summed
+        to_north[...] = summed[128:136, 128:] + pltpu.roll(summed[128:136, 128:], 4, 0)
+        to_south[...] = summed[0:8, :128] + pltpu.roll(summed[0:8, :128], 4, 0)
+
+    pl.run_scoped(accumulate, *[pltpu.ACC(m)((HPAD * 8, COLS), F32) for m in range(2)])
+
+    def drain(g, carry):
+        outgoing(g).wait()
+        return carry
+
+    lax.fori_loop(0, GROUPS, drain, 0)
+
+
+def sweep(vert, seed, surf, east, north, land, to_east, to_west, west, east_in, send_a, send_b, got_a, got_b,
+          weights, slots):
     whole = lambda *shape: pl.BlockSpec(shape, lambda i: (0,) * len(shape))
     tile = whole(ROWS, COLS)
     cols = whole(ROWS, 128)
     message = whole(4, MSG, 128)
-    plane = pl.BlockSpec((1, ROWS, COLS), lambda i: (i, 0, 0))
-    stack = pl.BlockSpec((1, LEV, ROWS, COLS), lambda i: (i, 0, 0, 0))
+    pair = whole(2, ROWS, COLS)
+    anywhere = pl.BlockSpec(memory_space=pl.ANY)
+    small = jax.ShapeDtypeStruct((8, 128), F32)
+    padded = pltpu.VMEM((LEV, ROWS + 16, COLS), F32)
     return pl.pallas_call(
-        step_body,
-        grid=(PL,),
-        in_specs=[pl.BlockSpec(memory_space=pltpu.SMEM), stack, plane, tile, tile, tile]
+        sweep_body,
+        grid=(1,),
+        in_specs=[pl.BlockSpec(memory_space=pltpu.SMEM), anywhere, whole(PL, ROWS, COLS), tile, tile, tile]
         + [cols] * 4
-        + [message] * 4,
-        out_specs=[stack, plane],
+        + [message] * 4
+        + [pair] * 2,
+        out_specs=[anywhere, whole(HPAD * 8, COLS), whole(8, 128), whole(8, 128)],
         out_shape=[
             jax.ShapeDtypeStruct((PL, LEV, ROWS, COLS), F32),
-            jax.ShapeDtypeStruct((PL, ROWS, COLS), F32),
+            jax.ShapeDtypeStruct((HPAD * 8, COLS), F32),
+            small,
+            small,
         ],
-        scratch_shapes=[
-            pltpu.VMEM((LEV, ROWS + 16, COLS), F32),
-            pltpu.VMEM((LEV, ROWS + 16, COLS), F32),
+        scratch_shapes=[padded] * 8
+        + [
+            pltpu.VMEM((PL, LEV, ROWS, COLS), F32),
+            pltpu.VMEM((PL, ROWS, COLS), F32),
             pltpu.VMEM((6, ROWS, COLS), F32),
-            pltpu.VMEM((2, LEV, ROWS, 128), F32),
+            pltpu.VMEM((2, PL, LEV, ROWS, 128), F32),
             pltpu.VMEM((ROWS, 128), F32),
             pltpu.VMEM((ROWS, 128), F32),
-            pltpu.VMEM((MSG, COLS), F32),
-            pltpu.VMEM((MSG, COLS), F32),
-            pltpu.VMEM((MSG, COLS), F32),
-            pltpu.VMEM((MSG, COLS), F32),
+        ]
+        + [pltpu.VMEM((MSG, COLS), F32)] * 4
+        + [
+            pltpu.VMEM((COLS, COLS), BF16),
+            pltpu.SemaphoreType.DMA((PL, GROUPS)),
+            pltpu.SemaphoreType.DMA((GROUPS,)),
         ],
         compiler_params=VM,
-        name="steps",
-    )(vert, seed, surf, east, north, land, to_east, to_west, west, east_in, send_a, send_b, got_a, got_b)
-
-
-def hot_low(ids):
-    grid = row_iota((COLS, ids.shape[1]))
-    return jnp.where(grid == (ids & 255), 1.0, 0.0).astype(BF16)
-
-
-def hot_high(ids, parts, count):
-    high = jnp.broadcast_to(ids >> 8, parts.shape)
-    return jnp.concatenate([jnp.where(high == h, parts, 0.0) for h in range(count)], axis=0).astype(BF16)
-
-
-def two_parts(values):
-    big = values.astype(BF16).astype(F32)
-    return jnp.concatenate([big, values - big], axis=0)
-
-
-CONTRACT = (((1,), (1,)), ((), ()))
-
-
-def spread_body(total, weights, slots, sums, to_north, to_south, grid_low):
-    grid_low[...] = row_iota((COLS, COLS)).astype(F32).astype(BF16)
-    which = (row_iota((16, COLS)) >> 3).astype(F32)
-    pairs = HPAD // 2
-
-    def accumulate(acc0, acc1):
-        accs = (acc0, acc1)
-
-        def block(i, carry):
-            rows = pl.ds(pl.multiple_of(i * 8, 8), 8)
-            ids_all = [slots[k, rows, :] for k in range(2)]
-            w_all = [weights[k, rows, :] for k in range(2)]
-            t_all = [total[p, rows, :] for p in range(PL)]
-            unit = 0
-            for r in range(8):
-                surface = jnp.concatenate([t[r : r + 1, :] for t in t_all], axis=0)
-                for k in range(2):
-                    ids = ids_all[k][r : r + 1, :]
-                    low = jnp.broadcast_to((ids & 255).astype(F32), (16, COLS)).astype(BF16)
-                    low = jnp.concatenate([low] * 16, axis=0)
-                    one_hot = jnp.where(grid_low[...] == low, jnp.array(1, BF16), jnp.array(0, BF16))
-                    parts = two_parts(surface * w_all[k][r : r + 1, :])
-                    parts = jnp.concatenate([parts, parts], axis=0).astype(BF16)
-                    high = jnp.broadcast_to((ids >> 8).astype(F32), (16, COLS)) - which
-                    high = high.astype(BF16)
-                    hot = jnp.concatenate(
-                        [jnp.where(high == jnp.array(2 * h, BF16), parts, jnp.array(0, BF16)) for h in range(pairs)],
-                        axis=0,
-                    )
-                    m = unit % 2
-                    reg = (unit // 2) % 2
-                    pltpu.matmul_push_rhs(one_hot, reg, m, transpose=True)
-                    pltpu.matmul_acc_lhs(accs[m], hot, load_staged_rhs=reg)
-                    unit += 1
-            return carry
-
-        lax.fori_loop(0, GROUPS, block, 0)
-        summed = pltpu.matmul_pop(acc0) + pltpu.matmul_pop(acc1)
-        sums[...] = summed
-        to_north[...] = summed[128:136, 128:] + pltpu.roll(summed[128:136, 128:], 4, 0)
-        to_south[...] = summed[0:8, :128] + pltpu.roll(summed[0:8, :128], 4, 0)
-
-    pl.run_scoped(accumulate, *[pltpu.ACC(m)((HPAD * 8, COLS), F32) for m in range(2)])
-
-
-def spread(total, weights, slots):
-    whole = lambda *shape: pl.BlockSpec(shape, lambda i: (0,) * len(shape))
-    small = jax.ShapeDtypeStruct((8, 128), F32)
-    return pl.pallas_call(
-        spread_body,
-        grid=(1,),
-        in_specs=[whole(PL, ROWS, COLS), whole(2, ROWS, COLS), whole(2, ROWS, COLS)],
-        out_specs=[whole(HPAD * 8, COLS), whole(8, 128), whole(8, 128)],
-        out_shape=[jax.ShapeDtypeStruct((HPAD * 8, COLS), F32), small, small],
-        scratch_shapes=[pltpu.VMEM((COLS, COLS), BF16)],
-        compiler_params=VM,
-        name="spread",
-    )(total, weights, slots)
+        name="sweep",
+    )(vert, seed, surf, east, north, land, to_east, to_west, west, east_in, send_a, send_b, got_a, got_b,
+      weights, slots)
 
 
 def gather_body(sums, south, north, serve, out):
@@ -595,15 +661,17 @@
     south_list = lax.ppermute(list_message(forcing_pert[:, -1], cells[-128:]), "lat", upward)
     north_list = lax.ppermute(list_message(forcing_pert[:, 0], cells[:128]), "lat", downward)
 
+    shift = ((fold_map[0] + 1) // COLS) % lon_count
+    shift, forcing = lax.optimization_barrier((shift, forcing_pert))
+
     surf, to_east, to_west, send_a, send_b = pick(
-        forcing_pert, serve_cells, south_list, north_list, ocean_slots, remap_weight,
+        forcing, serve_cells, south_list, north_list, ocean_slots, remap_weight,
         ocean_seed, east_coef, north_coef, land_mask,
     )
 
     west = lax.ppermute(to_east, "lon", eastward)
     east = lax.ppermute(to_west, "lon", westward)
     send_a, send_b = corners(west, east, send_a, send_b)
-    shift = ((fold_map[0] + 1) // COLS) % lon_count
     got_a = lax.ppermute(send_a, "lat", [(i ^ 1, i) for i in range(lat_count)])
     got_b = lax.switch(
         shift,
@@ -613,11 +681,10 @@
         ],
         send_b,
     )
-    adjoint_two, total = steps(
+    adjoint_two, sums, to_north, to_south = sweep(
         vert_coef, ocean_seed, surf, east_coef, north_coef, land_mask, to_east, to_west, west, east,
-        send_a, send_b, got_a, got_b,
+        send_a, send_b, got_a, got_b, remap_weight, ocean_slots,
     )
-    sums, to_north, to_south = spread(total, remap_weight, ocean_slots)
     from_south = lax.ppermute(to_north, "lat", upward)
     from_north = lax.ppermute(to_south, "lat", downward)
     stress_sens = gather(sums, from_south, from_north, serve_cells)

time: 98.9 us -> 89.8 us (0.908)
  Pallas kernels: 47.5 us -> 40.4 us
  starting transfers between devices: 30.3 us -> 28.5 us
    pallas_call x2 -> x1, Pallas kernels: 28.4 us -> 21.3 us  [sweep(): pl.pallas_call(sweep_body, grid=(1,), in_specs=[pl.BlockSpec(memory_space...]
    ppermute x1, waiting for transfers between devices: 1.29 us -> 0.01 us  [shards(): lax.ppermute(list_message(forcing_pert[:, -1], cells[-128:]), 'lat', upward)]
    ppermute x1, starting transfers between devices: 7.78 us -> 6.52 us  [shards(): lax.ppermute(v, ('lon', 'lat'), ladder(lon_count, lat_count, s))]
  transfers between devices with their start and end apart: 8 -> 8, of which waited for: 5 -> 4; matrix products, arithmetic and copies ran while one was open for 1% -> 1% of each run, Pallas kernels for 0% -> 0%
where the time goes in v1:
time: 89.8 us; the launch traced here: 89.4 us
  Pallas kernels  40.4 us (45%)
  starting transfers between devices  28.5 us (32%)
  waiting for transfers between devices  13.3 us (15%)
  local copies, waits for them, and re-layouts  5.02 us (6%)
  between operations  1.42 us (2%)
    pallas_call x1, Pallas kernels, sweep(): pl.pallas_call(sweep_body, grid=(1,), in_specs=[pl.BlockSpec(memory_space...  21.3 us
    pallas_call x1, Pallas kernels, pick(): pl.pallas_call(pick_body, grid=(ROWS // block,), in_specs=[whole(PL, 32,...  15.3 us
    ppermute x1, waiting for transfers between devices, shards(): from_north = lax.ppermute(to_south, 'lat', downward)  7.38 us
    ppermute x1, starting transfers between devices, shards(): lax.ppermute(list_message(forcing_pert[:, -1], cells[-128:]), 'lat', upward)  6.8 us
    ppermute x1, starting transfers between devices, shards(): from_south = lax.ppermute(to_north, 'lat', upward)  6.66 us
    ppermute x1, starting transfers between devices, shards(): lax.ppermute(v, ('lon', 'lat'), ladder(lon_count, lat_count, s))  6.52 us
    ppermute x1, starting transfers between devices, shards(): east = lax.ppermute(to_west, 'lon', westward)  3.91 us
    ppermute x1, waiting for transfers between devices, shards(): lax.ppermute(v, ('lon', 'lat'), ladder(lon_count, lat_count, s))  3.7 us
  transfers between devices with their start and end apart: 8, of which 4 were waited for; matrix products, arithmetic and copies ran while one was open for 1% of the time, Pallas kernels for 0%

profile of v1, /device:TPU:24, one launch (start us, length us, event | category | flops | bytes accessed | tf_op | source)
XLA Modules:
  0.0 89.4 jit_solution(1792701578875455789)
XLA Ops:
  0.6 0.7 slice_convert_fusion
  1.3 0.7 fusion
  2.0 0.1 pad.5.clone
  2.1 0.1 maximum_maximum_fusion.1
  2.2 2.6 %collective-permute-start.17 = (f32[8,128]{1,0:T(8,128)S(1)}, f32[8,128]{1,0:T(8,128)S(1)}, u32[]{:S(2)}, u32[]{:S(2)}) collective-permute-start(f32[8,128]{1,0:T(8,128)S(1)} %get-tuple-element.65), channel_id=1, source_target_pairs={{1,0},{2,1},{3,2},{4,3},{5,4},{6,5},{7,6},{9,8},{10,9},{11,10},{12... | collective-permute-start | bytes 12296 | tf_op jit(solution)/shard_map/ppermute | solution.py:662
  4.8 6.8 %collective-permute-start.16 = (f32[8,128]{1,0:T(8,128)S(1)}, f32[8,128]{1,0:T(8,128)S(1)}, u32[]{:S(2)}, u32[]{:S(2)}) collective-permute-start(f32[8,128]{1,0:T(8,128)S(1)} %get-tuple-element.66), channel_id=1, source_target_pairs={{0,1},{1,2},{2,3},{3,4},{4,5},{5,6},{6,7},{8,9},{9,10},{10,11},{11... | collective-permute-start | bytes 12296 | tf_op jit(solution)/shard_map/ppermute | solution.py:661
  11.7 1.2 %slice.17 = s32[1]{0:T(128)} slice(s32[4096]{0:T(1024)} %param.35), slice={[0:1]} | slice | bytes 8 | tf_op jit(solution)/shard_map/slice | solution.py:664
  13.5 0.0 collective-permute-done.17.north
  13.6 0.0 copy-start.5
  13.6 0.0 collective-permute-done.16.south
  13.6 0.6 copy-done.5
  14.2 0.0 copy-start.6
  14.2 0.6 copy-done.6
  14.7 15.3 %pick.1 = (f32[4,128,256]{2,1,0:T(8,128)}, f32[128,128]{1,0:T(8,128)}, f32[128,128]{1,0:T(8,128)}, f32[4,48,128]{2,1,0:T(8,128)}, f32[4,48,128]{2,1,0:T(8,128)S(1)}) custom-call(f32[4,32,128]{2,1,0:T(8,128)} %forcing, s32[1,4352]{1,0:T(1,128)} %serve.3, f32[8,128]{1,0:T(8,128)} %copy-done.6, f32[8,128]{1,0:T(8,128)} %copy-done.5, s32[2,128,256]{2,1,0:T(8,128)} %slots.3, ...), custom_call_target="tpu_custom_call" | custom-call | tf_op jit(solution)/shard_map/pick/pallas_call | solution.py:141
  30.1 0.1 collective-permute-start.18
  30.1 3.9 %collective-permute-start.19 = (f32[128,128]{1,0:T(8,128)}, f32[128,128]{1,0:T(8,128)S(1)}, u32[]{:S(2)}, u32[]{:S(2)}) collective-permute-start(f32[128,128]{1,0:T(8,128)} %get-tuple-element.51.to_west), channel_id=1, source_target_pairs={{8,0},{16,8},{24,16},{32,24},{40,32},{48,40},{56,48},{64,56},{72,6... | collective-permute-start | bytes 196616 | tf_op jit(solution)/shard_map/ppermute | solution.py:673
  34.1 2.1 %collective-permute-done.18.west_first.west_last.west0 = f32[128,128]{1,0:T(8,128)S(1)} collective-permute-done((f32[128,128]{1,0:T(8,128)}, f32[128,128]{1,0:T(8,128)S(1)}, u32[]{:S(2)}, u32[]{:S(2)}) %collective-permute-start.18) | collective-permute-done | bytes 65568 | tf_op jit(solution)/shard_map/ppermute | solution.py:672
  36.1 0.0 copy-start
  36.1 0.1 collective-permute-done.19.east_first.east_last.east0
  36.3 0.0 copy-start.1
  36.3 0.5 copy-done
  36.8 0.1 copy-done.1
  36.9 1.3 %corners.1 = (f32[4,48,128]{2,1,0:T(8,128)}, f32[4,48,128]{2,1,0:T(8,128)S(1)}) custom-call(f32[128,128]{1,0:T(8,128)} %copy-done, f32[128,128]{1,0:T(8,128)} %copy-done, f32[128,128]{1,0:T(8,128)} %copy-done.1, f32[128,128]{1,0:T(8,128)} %copy-done.1, f32[4,48,128]{2,1,0:T(8,128)} %get-tuple-element.52.tile_a, ...), custom_call_target="tpu_custom_call", output_to_operand_aliasing={{0}: (4, {}), {1}: (5, {})} | custom-call | tf_op jit(solution)/shard_map/corners/pallas_call | solution.py:183
  38.2 0.0 collective-permute-start.20
  38.2 10.2 %conditional.1 = (f32[4,48,128]{2,1,0:T(8,128)}) conditional(s32[]{:T(128)} %clamp.3, f32[4,48,128]{2,1,0:T(8,128)S(1)} %get-tuple-element.55.send_b, f32[4,48,128]{2,1,0:T(8,128)S(1)} %get-tuple-element.55.send_b, f32[4,48,128]{2,1,0:T(8,128)S(1)} %get-tuple-element.55.send_b, ...), branch_computations={%region_0.1_spmd, %region_1.2_spmd, %region_2.3_spmd, %region_3.4_... | conditional | bytes 393264 | solution.py:676
  38.2 6.5 %collective-permute-start.12 = (f32[4,48,128]{2,1,0:T(8,128)S(1)}, f32[4,48,128]{2,1,0:T(8,128)}, u32[]{:S(2)}, u32[]{:S(2)}) collective-permute-start(f32[4,48,128]{2,1,0:T(8,128)S(1)} %param.12), channel_id=1, source_target_pairs={{1,2},{2,1},{3,4},{4,3},{5,6},{6,5},{7,95},{9,10},{10,9},{11,12},{... | collective-permute-start | bytes 294920 | tf_op jit(solution)/shard_map/cond/branch_12_fun/ppermute | solution.py:679
  44.7 3.7 %collective-permute-done.12 = f32[4,48,128]{2,1,0:T(8,128)} collective-permute-done((f32[4,48,128]{2,1,0:T(8,128)S(1)}, f32[4,48,128]{2,1,0:T(8,128)}, u32[]{:S(2)}, u32[]{:S(2)}) %collective-permute-start.12) | collective-permute-done | bytes 98336 | tf_op jit(solution)/shard_map/cond/branch_12_fun/ppermute | solution.py:679
  48.4 0.0 collective-permute-done.20.got_a
  48.4 0.0 copy-start.2
  48.4 0.6 copy-done.2
  49.1 21.3 %sweep.1 = (f32[4,10,128,256]{3,2,1,0:T(8,128)}, f32[144,256]{1,0:T(8,128)}, f32[8,128]{1,0:T(8,128)}, f32[8,128]{1,0:T(8,128)}) custom-call(f32[9]{0:T(128)} %vert.1, f32[4,10,128,256]{3,2,1,0:T(8,128)} %seed.3, f32[4,128,256]{2,1,0:T(8,128)} %get-tuple-element.49.surf, f32[128,256]{1,0:T(8,128)} %east.3, f32[128,256]{1,0:T(8,128)} %north.1, ...), custom_call_target="tpu_custom_call" | custom-call | tf_op jit(solution)/shard_map/sweep/pallas_call | solution.py:564
  70.3 6.7 %collective-permute-start.21 = (f32[8,128]{1,0:T(8,128)}, f32[8,128]{1,0:T(8,128)S(1)}, u32[]{:S(2)}, u32[]{:S(2)}) collective-permute-start(f32[8,128]{1,0:T(8,128)} %get-tuple-element.59), channel_id=1, source_target_pairs={{0,1},{1,2},{2,3},{3,4},{4,5},{5,6},{6,7},{8,9},{9,10},{10,11},{11... | collective-permute-start | bytes 12296 | tf_op jit(solution)/shard_map/ppermute | solution.py:688
  77.0 1.9 %collective-permute-start.22 = (f32[8,128]{1,0:T(8,128)}, f32[8,128]{1,0:T(8,128)S(1)}, u32[]{:S(2)}, u32[]{:S(2)}) collective-permute-start(f32[8,128]{1,0:T(8,128)} %get-tuple-element.60), channel_id=1, source_target_pairs={{1,0},{2,1},{3,2},{4,3},{5,4},{6,5},{7,6},{9,8},{10,9},{11,10},{12... | collective-permute-start | bytes 12296 | tf_op jit(solution)/shard_map/ppermute | solution.py:689
  78.9 0.0 collective-permute-done.21.south
  78.9 0.0 copy-start.3
  78.9 7.4 %collective-permute-done.22.north = f32[8,128]{1,0:T(8,128)S(1)} collective-permute-done((f32[8,128]{1,0:T(8,128)}, f32[8,128]{1,0:T(8,128)S(1)}, u32[]{:S(2)}, u32[]{:S(2)}) %collective-permute-start.22) | collective-permute-done | bytes 4128 | tf_op jit(solution)/shard_map/ppermute | solution.py:689
  86.3 0.0 copy-start.4
  86.3 0.0 copy-done.3
  86.3 0.6 copy-done.4
  86.9 2.5 %gather.1 = f32[4,32,128]{2,1,0:T(8,128)} custom-call(f32[144,256]{1,0:T(8,128)} %get-tuple-element.58.sums, f32[8,128]{1,0:T(8,128)} %copy-done.3, f32[8,128]{1,0:T(8,128)} %copy-done.4, s32[1,4352]{1,0:T(1,128)} %serve.3), custom_call_target="tpu_custom_call" | custom-call | tf_op jit(solution)/shard_map/gather/pallas_call | solution.py:623
  (1 shorter events, 0.0 us)
Async XLA Ops:
  2.2 11.4 %collective-permute-start.17 = (f32[8,128]{1,0:T(8,128)S(1)}, f32[8,128]{1,0:T(8,128)S(1)}, u32[]{:S(2)}, u32[]{:S(2)}) collective-permute-start(f32[8,128]{1,0:T(8,128)S(1)} %get-tuple-element.65), channel_id=1, source_target_pairs={{1,0},{2,1},{3,2},{4,3},{5,4},{6,5},{7,6},{9,8},{10,9},{11,10},{12... | collective-permute-start | bytes 12296 | tf_op jit(solution)/shard_map/ppermute | solution.py:662
  4.8 8.7 %collective-permute-start.16 = (f32[8,128]{1,0:T(8,128)S(1)}, f32[8,128]{1,0:T(8,128)S(1)}, u32[]{:S(2)}, u32[]{:S(2)}) collective-permute-start(f32[8,128]{1,0:T(8,128)S(1)} %get-tuple-element.66), channel_id=1, source_target_pairs={{0,1},{1,2},{2,3},{3,4},{4,5},{5,6},{6,7},{8,9},{9,10},{10,11},{11... | collective-permute-start | bytes 12296 | tf_op jit(solution)/shard_map/ppermute | solution.py:661
  13.6 0.6 copy-start.5
  14.2 0.6 copy-start.6
  30.1 6.1 %collective-permute-start.18 = (f32[128,128]{1,0:T(8,128)}, f32[128,128]{1,0:T(8,128)S(1)}, u32[]{:S(2)}, u32[]{:S(2)}) collective-permute-start(f32[128,128]{1,0:T(8,128)} %get-tuple-element.50.to_east), channel_id=1, source_target_pairs={{0,8},{8,16},{16,24},{24,32},{32,40},{40,48},{48,56},{56,64},{64,7... | collective-permute-start | bytes 196616 | tf_op jit(solution)/shard_map/ppermute | solution.py:672
  30.1 6.1 %collective-permute-start.19 = (f32[128,128]{1,0:T(8,128)}, f32[128,128]{1,0:T(8,128)S(1)}, u32[]{:S(2)}, u32[]{:S(2)}) collective-permute-start(f32[128,128]{1,0:T(8,128)} %get-tuple-element.51.to_west), channel_id=1, source_target_pairs={{8,0},{16,8},{24,16},{32,24},{40,32},{48,40},{56,48},{64,56},{72,6... | collective-permute-start | bytes 196616 | tf_op jit(solution)/shard_map/ppermute | solution.py:673
  36.1 0.6 copy-start
  36.3 0.6 copy-start.1
  38.2 10.2 %collective-permute-start.20 = (f32[4,48,128]{2,1,0:T(8,128)}, f32[4,48,128]{2,1,0:T(8,128)S(1)}, u32[]{:S(2)}, u32[]{:S(2)}) collective-permute-start(f32[4,48,128]{2,1,0:T(8,128)} %get-tuple-element.54.send_a), channel_id=1, source_target_pairs={{1,0},{0,1},{3,2},{2,3},{5,4},{4,5},{7,6},{6,7},{9,8},{8,9},{11,10... | collective-permute-start | bytes 294920 | tf_op jit(solution)/shard_map/ppermute | solution.py:675
  38.2 10.2 %collective-permute-start.12 = (f32[4,48,128]{2,1,0:T(8,128)S(1)}, f32[4,48,128]{2,1,0:T(8,128)}, u32[]{:S(2)}, u32[]{:S(2)}) collective-permute-start(f32[4,48,128]{2,1,0:T(8,128)S(1)} %param.12), channel_id=1, source_target_pairs={{1,2},{2,1},{3,4},{4,3},{5,6},{6,5},{7,95},{9,10},{10,9},{11,12},{... | collective-permute-start | bytes 294920 | tf_op jit(solution)/shard_map/cond/branch_12_fun/ppermute | solution.py:679
  48.4 0.6 copy-start.2
  70.3 8.6 %collective-permute-start.21 = (f32[8,128]{1,0:T(8,128)}, f32[8,128]{1,0:T(8,128)S(1)}, u32[]{:S(2)}, u32[]{:S(2)}) collective-permute-start(f32[8,128]{1,0:T(8,128)} %get-tuple-element.59), channel_id=1, source_target_pairs={{0,1},{1,2},{2,3},{3,4},{4,5},{5,6},{6,7},{8,9},{9,10},{10,11},{11... | collective-permute-start | bytes 12296 | tf_op jit(solution)/shard_map/ppermute | solution.py:688
  77.0 9.3 %collective-permute-start.22 = (f32[8,128]{1,0:T(8,128)}, f32[8,128]{1,0:T(8,128)S(1)}, u32[]{:S(2)}, u32[]{:S(2)}) collective-permute-start(f32[8,128]{1,0:T(8,128)} %get-tuple-element.60), channel_id=1, source_target_pairs={{1,0},{2,1},{3,2},{4,3},{5,4},{6,5},{7,6},{9,8},{10,9},{11,10},{12... | collective-permute-start | bytes 12296 | tf_op jit(solution)/shard_map/ppermute | solution.py:689
  78.9 7.4 %copy-start.3 = (f32[8,128]{1,0:T(8,128)}, f32[8,128]{1,0:T(8,128)S(1)}, u32[]{:S(2)}) copy-start(f32[8,128]{1,0:T(8,128)S(1)} %collective-permute-done.21.south) | copy-start | bytes 12292
  86.3 0.6 copy-start.4

commit v2 on v1

--- a/solution.py
+++ b/solution.py
@@ -18,7 +18,7 @@
 F32 = jnp.float32
 BF16 = jnp.bfloat16
 GROUPS = ROWS // 8
-VM = pltpu.CompilerParams(vmem_limit_bytes=56 * 1024 * 1024)
+VM = pltpu.CompilerParams(vmem_limit_bytes=64 * 1024 * 1024)
 
 
 def lane_iota(shape):
@@ -34,132 +34,174 @@
     return jnp.take_along_axis(table, low, axis=1, mode="promise_in_bounds")
 
 
+BLOCK = 16
+
+
 def pick_body(
-    forcing, serve, south, north, slots, weights, seed, east, north_c, land,
-    surf, to_east, to_west, send_a, send_b, pool,
+    forcing, serve, south, north, slots, weights, seed_hbm, east, north_c, land,
+    surf, to_east, to_west, send_a, send_b,
+    seed, pool, table, halves, grid_low, left, right, arrive,
 ):
     even = lax.axis_index("lat") % 2 == 0
-    step = pl.program_id(0)
-    steps = pl.num_programs(0)
-
-    @pl.when(step == 0)
-    def _():
-        pool[:, LISTS:, :] = jnp.zeros((PL, 40 - LISTS, 128), F32)
-        for g in range(4):
-            ids = jnp.concatenate(
-                [serve[:, 128 * (8 * g + i + 1) : 128 * (8 * g + i + 2)] for i in range(8)], axis=0
-            )
-            low = ids & 127
-            high = ids >> 7
-            acc = [jnp.zeros((8, 128), F32) for _ in range(PL)]
-            for h in range(32):
-                hit = high == h
-                for p in range(PL):
-                    acc[p] = jnp.where(hit, lookup(forcing[p, h : h + 1, :], low), acc[p])
+
+    def incoming(i):
+        rows = pl.ds(pl.multiple_of(i * BLOCK, BLOCK), BLOCK)
+        return pltpu.make_async_copy(seed_hbm.at[:, :, rows, :], seed.at[:, :, rows, :], arrive.at[i])
+
+    def fetch(i, carry):
+        incoming(i).start()
+        return carry
+
+    lax.fori_loop(0, ROWS // BLOCK, fetch, 0)
+
+    pool[:, LISTS:, :] = jnp.zeros((PL, 40 - LISTS, 128), F32)
+    for g in range(4):
+        ids = jnp.concatenate(
+            [serve[:, 128 * (8 * g + i + 1) : 128 * (8 * g + i + 2)] for i in range(8)], axis=0
+        )
+        low = ids & 127
+        high = ids >> 7
+        acc = [jnp.zeros((8, 128), F32) for _ in range(PL)]
+        for h in range(32):
+            hit = high == h
             for p in range(PL):
-                pool[p, 1 + 8 * g : 9 + 8 * g, :] = acc[p]
-        for recv, place in ((south, 0), (north, LISTS - 1)):
-            low = jnp.broadcast_to(recv[4:5, :].astype(jnp.int32) & 127, (8, 128))
-            for p in range(PL):
-                got = lookup(recv[p : p + 1, :], low)
-                pool[p, place : place + 1, :] = got[0:1, :]
-
-    block = surf.shape[1]
+                acc[p] = jnp.where(hit, lookup(forcing[p, h : h + 1, :], low), acc[p])
+        for p in range(PL):
+            pool[p, 1 + 8 * g : 9 + 8 * g, :] = acc[p]
+    for recv, place in ((south, 0), (north, LISTS - 1)):
+        low = jnp.broadcast_to(recv[4:5, :].astype(jnp.int32) & 127, (8, 128))
+        for p in range(PL):
+            got = lookup(recv[p : p + 1, :], low)
+            pool[p, place : place + 1, :] = got[0:1, :]
+    for h in range(HPAD):
+        for t in range(2):
+            rows = jnp.concatenate([pool[p, 2 * h + t : 2 * h + t + 1, :] for p in range(PL)], axis=0)
+            halves[8 * h : 8 * h + 8, 128 * t : 128 * t + 128] = two_parts(rows)
+    table[...] = halves[...].astype(BF16)
+    grid_low[...] = row_iota((COLS, COLS)).astype(F32).astype(BF16)
+
     lanes = lane_iota((8, 128))
-    for g in range(block // 8):
-        rs = slice(8 * g, 8 * g + 8)
-        image = []
-        for t in range(2):
-            cs = slice(128 * t, 128 * t + 128)
-            acc = []
-            for k in range(2):
-                ids = slots[k, rs, cs]
+    pair = lanes >> 1
+    tiles = (slice(0, 128), slice(128, 256))
+    statics = (east, north_c, land)
+
+    def images(*accs):
+        def body(i, carry):
+            incoming(i).wait()
+            groups = [pl.ds(pl.multiple_of(i * BLOCK + 8 * g, 8), 8) for g in range(BLOCK // 8)]
+            ids_one = [slots[1, rs, :] for rs in groups]
+            w_one = [weights[1, rs, :] for rs in groups]
+
+            def issue(r):
+                ids = ids_one[r // 8][r % 8 : r % 8 + 1, :]
+                low = jnp.broadcast_to((ids & 255).astype(F32), (16, COLS)).astype(BF16)
+                low = jnp.concatenate([low] * 16, axis=0)
+                one_hot = jnp.where(grid_low[...] == low, jnp.array(1, BF16), jnp.array(0, BF16))
+                pltpu.matmul_push_rhs(one_hot, (r // 2) % 2, r % 2)
+                pltpu.matmul_acc_lhs(accs[r % 4], table[...], load_staged_rhs=(r // 2) % 2)
+
+            def collect(r):
+                got = pltpu.matmul_pop(accs[r % 4])
+                high = jnp.broadcast_to(ids_one[r // 8][r % 8 : r % 8 + 1, :] >> 8, (8, COLS))
+                mine = jnp.zeros((8, COLS), F32)
+                for h in range(HI):
+                    mine = jnp.where(high == h, got[8 * h : 8 * h + 8, :], mine)
+                mine = (mine + pltpu.roll(mine, 4, 0)) * w_one[r // 8][r % 8 : r % 8 + 1, :]
+                left[8 * r : 8 * r + 8, :] = mine[:, :128]
+                right[8 * r : 8 * r + 8, :] = mine[:, 128:]
+
+            zero = []
+            for unit in range(BLOCK // 4):
+                g, t = divmod(unit, 2)
+                ids = slots[0, groups[g], tiles[t]]
                 low = ids & 127
                 high = ids >> 7
                 own = [jnp.zeros((8, 128), F32) for _ in range(PL)]
                 for h in range(LISTS):
+                    if h % 8 == 0 and h < 32:
+                        r = 4 * unit + h // 8
+                        issue(r)
+                        if r >= 2:
+                            collect(r - 2)
                     hit = high == h
                     for p in range(PL):
                         own[p] = jnp.where(hit, lookup(pool[p, h : h + 1, :], low), own[p])
-                acc.append(own)
-            image.append(
-                [weights[0, rs, cs] * acc[0][p] + weights[1, rs, cs] * acc[1][p] for p in range(PL)]
-            )
-        for p in range(PL):
-            surf[p, rs, 0:128] = image[0][p]
-            surf[p, rs, 128:256] = image[1][p]
-        pair = lanes >> 1
-        statics = (east, north_c, land)
-        for t, out, first in ((0, to_west, 0), (1, to_east, 126)):
-            cs = slice(128 * t, 128 * t + 128)
-            acc = jnp.zeros((8, 128), F32)
-            for m in range(NPL + 3):
-                if m < NPL:
-                    p, k = divmod(m, LEV)
-                    v = seed[p, k, rs, cs]
-                    if k == 0:
-                        v = v + image[t][p]
-                else:
-                    v = statics[m - NPL][rs, cs].astype(F32)
-                shift = (2 * m - first) % 128
-                if shift:
-                    v = pltpu.roll(v, shift, 1)
-                acc = jnp.where(pair == m, v, acc)
-            out[rs, :] = acc
+                zero.append([weights[0, groups[g], tiles[t]] * own[p] for p in range(PL)])
+            collect(BLOCK - 2)
+            collect(BLOCK - 1)
+
+            for g, rs in enumerate(groups):
+                for t, part, out, first in ((0, left, to_west, 0), (1, right, to_east, 126)):
+                    image = []
+                    for p in range(PL):
+                        image.append(zero[2 * g + t][p] + part[pl.ds(64 * g + p, 8, stride=8), :])
+                        surf[p, rs, tiles[t]] = image[p]
+                    acc = jnp.zeros((8, 128), F32)
+                    for m in range(NPL + 3):
+                        if m < NPL:
+                            p, k = divmod(m, LEV)
+                            v = seed[p, k, rs, tiles[t]]
+                            if k == 0:
+                                v = v + image[p]
+                        else:
+                            v = statics[m - NPL][rs, tiles[t]].astype(F32)
+                        shift = (2 * m - first) % 128
+                        if shift:
+                            v = pltpu.roll(v, shift, 1)
+                        acc = jnp.where(pair == m, v, acc)
+                    out[rs, :] = acc
+            return carry
+
+        lax.fori_loop(0, ROWS // BLOCK, body, 0)
+
+    pl.run_scoped(images, *[pltpu.ACC(m % 2)((HPAD * 8, COLS), F32) for m in range(4)])
 
     def rows_out(out, adjacent, second):
         out[...] = jnp.zeros_like(out)
         for c, r in ((0, adjacent), (1, second)):
             for t in range(2):
-                cs = slice(128 * t, 128 * t + 128)
                 for m in range(NPL):
                     p, k = divmod(m, LEV)
-                    v = seed[p, k, r : r + 1, cs]
+                    v = seed[p, k, r : r + 1, tiles[t]]
                     if k == 0:
-                        v = v + surf[p, r : r + 1, cs]
+                        v = v + surf[p, r : r + 1, tiles[t]]
                     out[2 * c + t, m : m + 1, :] = v
-                out[2 * c + t, 40:41, :] = east[r : r + 1, cs]
-                out[2 * c + t, 41:42, :] = north_c[r : r + 1, cs]
-                out[2 * c + t, 42:43, :] = land[r : r + 1, cs].astype(F32)
+                out[2 * c + t, 40:41, :] = east[r : r + 1, tiles[t]]
+                out[2 * c + t, 41:42, :] = north_c[r : r + 1, tiles[t]]
+                out[2 * c + t, 42:43, :] = land[r : r + 1, tiles[t]].astype(F32)
 
     for flag, low_out, high_out in ((even, send_b, send_a), (jnp.logical_not(even), send_a, send_b)):
 
-        @pl.when(jnp.logical_and(flag, step == 0))
+        @pl.when(flag)
         def _():
             rows_out(low_out, 0, 1)
-
-        @pl.when(jnp.logical_and(flag, step == steps - 1))
-        def _():
-            rows_out(high_out, block - 1, block - 2)
+            rows_out(high_out, ROWS - 1, ROWS - 2)
 
 
 def pick(forcing, serve, south, north, slots, weights, seed, east, north_c, land):
-    block = 16
     whole = lambda *shape: pl.BlockSpec(shape, lambda i: (0,) * len(shape))
-    tile = pl.BlockSpec((block, COLS), lambda i: (i, 0))
-    pair = pl.BlockSpec((2, block, COLS), lambda i: (0, i, 0))
+    tile = whole(ROWS, COLS)
+    pair = whole(2, ROWS, COLS)
+    shapes = [(PL, ROWS, COLS), (ROWS, 128), (ROWS, 128), (4, MSG, 128), (4, MSG, 128)]
     return pl.pallas_call(
         pick_body,
-        grid=(ROWS // block,),
+        grid=(1,),
         in_specs=[
             whole(PL, 32, 128), whole(1, LISTS * 128), whole(8, 128), whole(8, 128), pair, pair,
-            pl.BlockSpec((PL, LEV, block, COLS), lambda i: (0, 0, i, 0)), tile, tile, tile,
+            pl.BlockSpec(memory_space=pl.ANY), tile, tile, tile,
         ],
-        out_specs=[
-            pl.BlockSpec((PL, block, COLS), lambda i: (0, i, 0)),
-            pl.BlockSpec((block, 128), lambda i: (i, 0)),
-            pl.BlockSpec((block, 128), lambda i: (i, 0)),
-            whole(4, MSG, 128),
-            whole(4, MSG, 128),
+        out_specs=[whole(*shape) for shape in shapes],
+        out_shape=[jax.ShapeDtypeStruct(shape, F32) for shape in shapes],
+        scratch_shapes=[
+            pltpu.VMEM((PL, LEV, ROWS, COLS), F32),
+            pltpu.VMEM((PL, 40, 128), F32),
+            pltpu.VMEM((HPAD * 8, COLS), BF16),
+            pltpu.VMEM((HPAD * 8, COLS), F32),
+            pltpu.VMEM((COLS, COLS), BF16),
+            pltpu.VMEM((8 * BLOCK, 128), F32),
+            pltpu.VMEM((8 * BLOCK, 128), F32),
+            pltpu.SemaphoreType.DMA((ROWS // BLOCK,)),
         ],
-        out_shape=[
-            jax.ShapeDtypeStruct((PL, ROWS, COLS), F32),
-            jax.ShapeDtypeStruct((ROWS, 128), F32),
-            jax.ShapeDtypeStruct((ROWS, 128), F32),
-            jax.ShapeDtypeStruct((4, MSG, 128), F32),
-            jax.ShapeDtypeStruct((4, MSG, 128), F32),
-        ],
-        scratch_shapes=[pltpu.VMEM((PL, 40, 128), F32)],
         compiler_params=VM,
         name="pick",
     )(forcing, serve, south, north, slots, weights, seed, east, north_c, land)

time: 89.8 us -> 84.3 us (0.939)
  Pallas kernels: 40.4 us -> 36.2 us
  local copies, waits for them, and re-layouts: 5.02 us -> 3.22 us
    pallas_call x1, Pallas kernels: 15.3 us -> 11.1 us  [pick(): pl.pallas_call(pick_body, grid=(1,), in_specs=[whole(PL, 32, 128), whole(...]
    unnamed x14 -> x6, local copies, waits for them, and re-layouts: 3 us -> 1.21 us
where the time goes in v2:
time: 84.3 us; the launch traced here: 83.9 us
  Pallas kernels  36.2 us (43%)
  starting transfers between devices  28.8 us (34%)
  waiting for transfers between devices  13.5 us (16%)
  local copies, waits for them, and re-layouts  3.22 us (4%)
  between operations  1.41 us (2%)
    pallas_call x1, Pallas kernels, sweep(): pl.pallas_call(sweep_body, grid=(1,), in_specs=[pl.BlockSpec(memory_space...  21.3 us
    pallas_call x1, Pallas kernels, pick(): pl.pallas_call(pick_body, grid=(1,), in_specs=[whole(PL, 32, 128), whole(...  11.1 us
    ppermute x1, waiting for transfers between devices, shards(): from_north = lax.ppermute(to_south, 'lat', downward)  7.49 us
    ppermute x1, starting transfers between devices, shards(): lax.ppermute(list_message(forcing_pert[:, -1], cells[-128:]), 'lat', upward)  6.81 us
    ppermute x1, starting transfers between devices, shards(): from_south = lax.ppermute(to_north, 'lat', upward)  6.77 us
    ppermute x1, starting transfers between devices, shards(): lax.ppermute(v, ('lon', 'lat'), ladder(lon_count, lat_count, s))  6.65 us
    ppermute x1, starting transfers between devices, shards(): east = lax.ppermute(to_west, 'lon', westward)  3.9 us
    ppermute x1, waiting for transfers between devices, shards(): lax.ppermute(v, ('lon', 'lat'), ladder(lon_count, lat_count, s))  3.79 us
  transfers between devices with their start and end apart: 8, of which 4 were waited for; matrix products, arithmetic and copies ran while one was open for 1% of the time, Pallas kernels for 0%

profile of v2, /device:TPU:24, one launch (start us, length us, event | category | flops | bytes accessed | tf_op | source)
XLA Modules:
  0.0 83.9 jit_solution(8860351783596366566)
XLA Ops:
  0.6 0.7 slice_convert_fusion
  1.3 0.7 fusion
  2.0 0.1 pad.5.clone
  2.1 0.1 maximum_maximum_fusion.1
  2.2 2.6 %collective-permute-start.17 = (f32[8,128]{1,0:T(8,128)S(1)}, f32[8,128]{1,0:T(8,128)S(1)}, u32[]{:S(2)}, u32[]{:S(2)}) collective-permute-start(f32[8,128]{1,0:T(8,128)S(1)} %get-tuple-element.65), channel_id=1, source_target_pairs={{1,0},{2,1},{3,2},{4,3},{5,4},{6,5},{7,6},{9,8},{10,9},{11,10},{12... | collective-permute-start | bytes 12296 | tf_op jit(solution)/shard_map/ppermute | solution.py:704
  4.8 6.8 %collective-permute-start.16 = (f32[8,128]{1,0:T(8,128)S(1)}, f32[8,128]{1,0:T(8,128)}, u32[]{:S(2)}, u32[]{:S(2)}) collective-permute-start(f32[8,128]{1,0:T(8,128)S(1)} %get-tuple-element.66), channel_id=1, source_target_pairs={{0,1},{1,2},{2,3},{3,4},{4,5},{5,6},{6,7},{8,9},{9,10},{10,11},{11... | collective-permute-start | bytes 12296 | tf_op jit(solution)/shard_map/ppermute | solution.py:703
  11.7 1.2 %slice.17 = s32[1]{0:T(128)} slice(s32[4096]{0:T(1024)} %param.35), slice={[0:1]} | slice | bytes 8 | tf_op jit(solution)/shard_map/slice | solution.py:706
  13.5 0.0 collective-permute-done.17.north
  13.6 0.0 copy-start.2
  13.6 0.6 copy-done.2
  14.2 0.0 collective-permute-done.16.south
  14.2 11.1 %pick.1 = (f32[4,128,256]{2,1,0:T(8,128)}, f32[128,128]{1,0:T(8,128)}, f32[128,128]{1,0:T(8,128)}, f32[4,48,128]{2,1,0:T(8,128)}, f32[4,48,128]{2,1,0:T(8,128)}) custom-call(f32[4,32,128]{2,1,0:T(8,128)} %forcing, s32[1,4352]{1,0:T(1,128)} %serve.3, f32[8,128]{1,0:T(8,128)} %collective-permute-done.16.south, f32[8,128]{1,0:T(8,128)} %copy-done.2, ...), custom_call_target="tpu_custom_call" | custom-call | tf_op jit(solution)/shard_map/pick/pallas_call | solution.py:186
  25.3 0.1 collective-permute-start.18
  25.4 3.9 %collective-permute-start.19 = (f32[128,128]{1,0:T(8,128)}, f32[128,128]{1,0:T(8,128)S(1)}, u32[]{:S(2)}, u32[]{:S(2)}) collective-permute-start(f32[128,128]{1,0:T(8,128)} %get-tuple-element.51.to_west), channel_id=1, source_target_pairs={{8,0},{16,8},{24,16},{32,24},{40,32},{48,40},{56,48},{64,56},{72,6... | collective-permute-start | bytes 196616 | tf_op jit(solution)/shard_map/ppermute | solution.py:715
  29.3 2.1 %collective-permute-done.18.west_first.west_last.west0 = f32[128,128]{1,0:T(8,128)S(1)} collective-permute-done((f32[128,128]{1,0:T(8,128)}, f32[128,128]{1,0:T(8,128)S(1)}, u32[]{:S(2)}, u32[]{:S(2)}) %collective-permute-start.18) | collective-permute-done | bytes 65568 | tf_op jit(solution)/shard_map/ppermute | solution.py:714
  31.4 0.0 copy-start
  31.4 0.1 collective-permute-done.19.east_first.east_last.east0
  31.5 0.0 copy-start.1
  31.5 0.5 copy-done
  32.0 0.1 copy-done.1
  32.1 1.3 %corners.1 = (f32[4,48,128]{2,1,0:T(8,128)}, f32[4,48,128]{2,1,0:T(8,128)}) custom-call(f32[128,128]{1,0:T(8,128)} %copy-done, f32[128,128]{1,0:T(8,128)} %copy-done, f32[128,128]{1,0:T(8,128)} %copy-done.1, f32[128,128]{1,0:T(8,128)} %copy-done.1, f32[4,48,128]{2,1,0:T(8,128)} %get-tuple-element.52.tile_a, ...), custom_call_target="tpu_custom_call", output_to_operand_aliasing={{0}: (4, {}), {1}: (5, {})} | custom-call | tf_op jit(solution)/shard_map/corners/pallas_call | solution.py:225
  33.4 0.0 collective-permute-start.20
  33.4 10.5 %conditional.1 = (f32[4,48,128]{2,1,0:T(8,128)}) conditional(s32[]{:T(128)} %clamp.3, f32[4,48,128]{2,1,0:T(8,128)} %get-tuple-element.55.send_b, f32[4,48,128]{2,1,0:T(8,128)} %get-tuple-element.55.send_b, f32[4,48,128]{2,1,0:T(8,128)} %get-tuple-element.55.send_b, ...), branch_computations={%region_0.1_spmd, %region_1.2_spmd, %region_2.3_spmd, %region_3.4_... | conditional | bytes 393264 | solution.py:718
  33.4 6.7 %collective-permute-start.9 = (f32[4,48,128]{2,1,0:T(8,128)}, f32[4,48,128]{2,1,0:T(8,128)}, u32[]{:S(2)}, u32[]{:S(2)}) collective-permute-start(f32[4,48,128]{2,1,0:T(8,128)} %param.9), channel_id=1, source_target_pairs={{1,2},{2,1},{3,4},{4,3},{5,6},{6,5},{7,71},{9,10},{10,9},{11,12},{... | collective-permute-start | bytes 294920 | tf_op jit(solution)/shard_map/cond/branch_9_fun/ppermute | solution.py:721
  40.1 3.8 %collective-permute-done.9 = f32[4,48,128]{2,1,0:T(8,128)} collective-permute-done((f32[4,48,128]{2,1,0:T(8,128)}, f32[4,48,128]{2,1,0:T(8,128)}, u32[]{:S(2)}, u32[]{:S(2)}) %collective-permute-start.9) | collective-permute-done | bytes 98336 | tf_op jit(solution)/shard_map/cond/branch_9_fun/ppermute | solution.py:721
  43.9 0.0 collective-permute-done.20.got_a
  43.9 21.3 %sweep.1 = (f32[4,10,128,256]{3,2,1,0:T(8,128)}, f32[144,256]{1,0:T(8,128)}, f32[8,128]{1,0:T(8,128)}, f32[8,128]{1,0:T(8,128)}) custom-call(f32[9]{0:T(128)} %vert.1, f32[4,10,128,256]{3,2,1,0:T(8,128)} %seed.1, f32[4,128,256]{2,1,0:T(8,128)} %get-tuple-element.49.surf, f32[128,256]{1,0:T(8,128)} %east.3, f32[128,256]{1,0:T(8,128)} %north.1, ...), custom_call_target="tpu_custom_call" | custom-call | tf_op jit(solution)/shard_map/sweep/pallas_call | solution.py:606
  65.2 6.8 %collective-permute-start.21 = (f32[8,128]{1,0:T(8,128)}, f32[8,128]{1,0:T(8,128)}, u32[]{:S(2)}, u32[]{:S(2)}) collective-permute-start(f32[8,128]{1,0:T(8,128)} %get-tuple-element.59), channel_id=1, source_target_pairs={{0,1},{1,2},{2,3},{3,4},{4,5},{5,6},{6,7},{8,9},{9,10},{10,11},{11... | collective-permute-start | bytes 12296 | tf_op jit(solution)/shard_map/ppermute | solution.py:730
  72.0 1.9 %collective-permute-start.22 = (f32[8,128]{1,0:T(8,128)}, f32[8,128]{1,0:T(8,128)}, u32[]{:S(2)}, u32[]{:S(2)}) collective-permute-start(f32[8,128]{1,0:T(8,128)} %get-tuple-element.60), channel_id=1, source_target_pairs={{1,0},{2,1},{3,2},{4,3},{5,4},{6,5},{7,6},{9,8},{10,9},{11,10},{12... | collective-permute-start | bytes 12296 | tf_op jit(solution)/shard_map/ppermute | solution.py:731
  73.9 0.0 collective-permute-done.21.south
  73.9 7.5 %collective-permute-done.22.north = f32[8,128]{1,0:T(8,128)} collective-permute-done((f32[8,128]{1,0:T(8,128)}, f32[8,128]{1,0:T(8,128)}, u32[]{:S(2)}, u32[]{:S(2)}) %collective-permute-start.22) | collective-permute-done | bytes 4128 | tf_op jit(solution)/shard_map/ppermute | solution.py:731
  81.4 2.5 %gather.1 = f32[4,32,128]{2,1,0:T(8,128)} custom-call(f32[144,256]{1,0:T(8,128)} %get-tuple-element.58.sums, f32[8,128]{1,0:T(8,128)} %collective-permute-done.21.south, f32[8,128]{1,0:T(8,128)} %collective-permute-done.22.north, s32[1,4352]{1,0:T(1,128)} %serve.3), custom_call_target="tpu_custom_call" | custom-call | tf_op jit(solution)/shard_map/gather/pallas_call | solution.py:665
  (1 shorter events, 0.0 us)
Async XLA Ops:
  2.2 11.4 %collective-permute-start.17 = (f32[8,128]{1,0:T(8,128)S(1)}, f32[8,128]{1,0:T(8,128)S(1)}, u32[]{:S(2)}, u32[]{:S(2)}) collective-permute-start(f32[8,128]{1,0:T(8,128)S(1)} %get-tuple-element.65), channel_id=1, source_target_pairs={{1,0},{2,1},{3,2},{4,3},{5,4},{6,5},{7,6},{9,8},{10,9},{11,10},{12... | collective-permute-start | bytes 12296 | tf_op jit(solution)/shard_map/ppermute | solution.py:704
  4.8 9.3 %collective-permute-start.16 = (f32[8,128]{1,0:T(8,128)S(1)}, f32[8,128]{1,0:T(8,128)}, u32[]{:S(2)}, u32[]{:S(2)}) collective-permute-start(f32[8,128]{1,0:T(8,128)S(1)} %get-tuple-element.66), channel_id=1, source_target_pairs={{0,1},{1,2},{2,3},{3,4},{4,5},{5,6},{6,7},{8,9},{9,10},{10,11},{11... | collective-permute-start | bytes 12296 | tf_op jit(solution)/shard_map/ppermute | solution.py:703
  13.6 0.6 copy-start.2
  25.3 6.1 %collective-permute-start.18 = (f32[128,128]{1,0:T(8,128)}, f32[128,128]{1,0:T(8,128)S(1)}, u32[]{:S(2)}, u32[]{:S(2)}) collective-permute-start(f32[128,128]{1,0:T(8,128)} %get-tuple-element.50.to_east), channel_id=1, source_target_pairs={{0,8},{8,16},{16,24},{24,32},{32,40},{40,48},{48,56},{56,64},{64,7... | collective-permute-start | bytes 196616 | tf_op jit(solution)/shard_map/ppermute | solution.py:714
  25.4 6.1 %collective-permute-start.19 = (f32[128,128]{1,0:T(8,128)}, f32[128,128]{1,0:T(8,128)S(1)}, u32[]{:S(2)}, u32[]{:S(2)}) collective-permute-start(f32[128,128]{1,0:T(8,128)} %get-tuple-element.51.to_west), channel_id=1, source_target_pairs={{8,0},{16,8},{24,16},{32,24},{40,32},{48,40},{56,48},{64,56},{72,6... | collective-permute-start | bytes 196616 | tf_op jit(solution)/shard_map/ppermute | solution.py:715
  31.4 0.6 copy-start
  31.5 0.6 copy-start.1
  33.4 10.5 %collective-permute-start.20 = (f32[4,48,128]{2,1,0:T(8,128)}, f32[4,48,128]{2,1,0:T(8,128)}, u32[]{:S(2)}, u32[]{:S(2)}) collective-permute-start(f32[4,48,128]{2,1,0:T(8,128)} %get-tuple-element.54.send_a), channel_id=1, source_target_pairs={{1,0},{0,1},{3,2},{2,3},{5,4},{4,5},{7,6},{6,7},{9,8},{8,9},{11,10... | collective-permute-start | bytes 294920 | tf_op jit(solution)/shard_map/ppermute | solution.py:717
  33.4 10.4 %collective-permute-start.9 = (f32[4,48,128]{2,1,0:T(8,128)}, f32[4,48,128]{2,1,0:T(8,128)}, u32[]{:S(2)}, u32[]{:S(2)}) collective-permute-start(f32[4,48,128]{2,1,0:T(8,128)} %param.9), channel_id=1, source_target_pairs={{1,2},{2,1},{3,4},{4,3},{5,6},{6,5},{7,71},{9,10},{10,9},{11,12},{... | collective-permute-start | bytes 294920 | tf_op jit(solution)/shard_map/cond/branch_9_fun/ppermute | solution.py:721
  65.2 8.7 %collective-permute-start.21 = (f32[8,128]{1,0:T(8,128)}, f32[8,128]{1,0:T(8,128)}, u32[]{:S(2)}, u32[]{:S(2)}) collective-permute-start(f32[8,128]{1,0:T(8,128)} %get-tuple-element.59), channel_id=1, source_target_pairs={{0,1},{1,2},{2,3},{3,4},{4,5},{5,6},{6,7},{8,9},{9,10},{10,11},{11... | collective-permute-start | bytes 12296 | tf_op jit(solution)/shard_map/ppermute | solution.py:730
  72.0 9.4 %collective-permute-start.22 = (f32[8,128]{1,0:T(8,128)}, f32[8,128]{1,0:T(8,128)}, u32[]{:S(2)}, u32[]{:S(2)}) collective-permute-start(f32[8,128]{1,0:T(8,128)} %get-tuple-element.60), channel_id=1, source_target_pairs={{1,0},{2,1},{3,2},{4,3},{5,4},{6,5},{7,6},{9,8},{10,9},{11,10},{12... | collective-permute-start | bytes 12296 | tf_op jit(solution)/shard_map/ppermute | solution.py:731
